TPU v7x, 128 devices: a whole 4x4x4 slice. The times are simulated.
128 devices in a mesh: dp: 4 (over y), mp: 32 (over x, z, core).
Axes of the slice: x: 4, y: 4, z: 4, core: 2. Of those that a mesh axis runs over, the one named last changes fastest.
Arguments:
- inputs: bfloat16 [2048, 4096], P('dp'), may hold values from -6 to 6
- out_grads: bfloat16 [2048, 4096], P('dp'), may hold values from -0.3984375 to 0.3984375
- w_gate: bfloat16 [4096, 11008], P(None, 'mp'), may hold values from -0.09375 to 0.09375
- w_up: bfloat16 [4096, 11008], P(None, 'mp'), may hold values from -0.09375 to 0.09375
- w_down: bfloat16 [11008, 4096], P('mp'), may hold values from -0.0546875 to 0.0546875
- err_down: bfloat16 [4, 11008, 4096], P('dp', 'mp'), may hold values from -3 to 3
- mom_down: float32 [11008, 4096], P('mp', 'dp'), may hold values from -0.3 to 0.3
- q_down: float32 [4096, 8], replicated, may hold values from -5 to 5
Outputs:
- in_grads: bfloat16 [2048, 4096], P('dp', 'mp')
- new_down: bfloat16 [11008, 4096], P('mp')
- next_err_down: bfloat16 [4, 11008, 4096], P('dp', 'mp')
- next_mom_down: float32 [11008, 4096], P('mp', 'dp')
All inputs are finite; a program needn't handle non-finite values.
Results may differ from a plain program's by a relative error of at most 0.005.
Values may be sent and summed in bfloat16 or wider, within the bound.
A program may use at most 128 MiB of HBM per device.

v0:
```python
import jax
import jax.numpy as jnp
from jax import lax
from jax.sharding import PartitionSpec as P

R = 8


HIGH = lax.Precision.HIGHEST


def orthonormal_split(panel):
    finished = []
    for col in range(R):
        vector = panel[:, col]
        if col > 0:
            basis = jnp.stack(finished, 1)
            coeffs = lax.psum(jnp.dot(basis.T, vector, precision=HIGH), "mp")
            vector = vector - jnp.dot(basis, coeffs, precision=HIGH)
        total = lax.psum(jnp.sum(vector * vector), "mp")
        vector = vector * lax.rsqrt(total + 1e-06)
        finished.append(vector)
    return jnp.stack(finished, 1)


def contract_rows(left, right):
    return lax.dot_general(
        left, right, (((0,), (0,)), ((), ())), preferred_element_type=jnp.float32
    )


def contract_cols(left, right):
    return lax.dot_general(
        left, right, (((1,), (1,)), ((), ())), preferred_element_type=jnp.float32
    )


def body(inputs, out_grads, w_gate, w_up, w_down, err_down, mom_down, q_down):
    replicas = lax.axis_size("dp")
    rank_dp = lax.axis_index("dp")
    gate = jnp.dot(inputs, w_gate, preferred_element_type=jnp.float32)
    up_val = jnp.dot(inputs, w_up, preferred_element_type=jnp.float32)
    sig = jax.nn.sigmoid(gate)
    hidden = (gate * sig * up_val).astype(jnp.bfloat16)
    d_hidden = contract_cols(out_grads, w_down)
    d_gate = (d_hidden * up_val * sig * (1.0 + gate * (1.0 - sig))).astype(jnp.bfloat16)
    d_up = (d_hidden * gate * sig).astype(jnp.bfloat16)
    partial_sum = contract_cols(d_gate, w_gate) + contract_cols(d_up, w_up)
    in_grads = lax.psum_scatter(partial_sum, "mp", scatter_dimension=1, tiled=True).astype(
        jnp.bfloat16
    )
    m_down = contract_rows(hidden, out_grads) + err_down[0].astype(jnp.float32)
    left_down = lax.psum(jnp.dot(m_down, q_down, precision=HIGH), "dp")
    left_down = orthonormal_split(left_down / replicas)
    right_down = lax.psum(contract_rows(m_down, left_down), ("dp", "mp"))
    approx_down = jnp.dot(left_down, right_down.T / replicas, precision=HIGH)
    next_err_down = (m_down - approx_down).astype(jnp.bfloat16)[None]
    cols = mom_down.shape[1]
    start = rank_dp * cols
    next_mom_down = 0.9 * mom_down + lax.dynamic_slice_in_dim(approx_down, start, cols, 1)
    own_down = (
        lax.dynamic_slice_in_dim(w_down, start, cols, 1).astype(jnp.float32) - 0.1 * next_mom_down
    ).astype(jnp.bfloat16)
    new_down = lax.all_gather(own_down, "dp", axis=1, tiled=True)
    return (in_grads, new_down, next_err_down, next_mom_down)


def solution(mesh):
    in_specs = (
        P("dp", None),
        P("dp", None),
        P(None, "mp"),
        P(None, "mp"),
        P("mp", None),
        P("dp", "mp", None),
        P("mp", "dp"),
        P(),
    )
    out_specs = (P("dp", "mp"), P("mp", None), P("dp", "mp", None), P("mp", "dp"))
    return jax.shard_map(body, mesh=mesh, in_specs=in_specs, out_specs=out_specs, check_vma=False)
```

profile of v0, /device:TPU:0, one launch (start us, length us, event | category | flops | bytes accessed | tf_op | source)
XLA Modules:
  0.0 1285.7 jit_solution(8486643587172567497)
XLA Ops:
  8.1 1.7 copy-done
  9.8 4.0 fusion.39
  13.8 0.3 copy-done.13
  14.1 1.7 fusion.38
  15.8 0.4 copy-done.3
  16.3 0.9 copy-done.4
  17.2 1.7 convolution_add_fusion.1
  19.0 2.5 copy-done.1
  21.5 4.5 fusion.40
  26.0 17.2 %psum.119 = f32[344,8]{0,1:T(8,128)S(1)} all-reduce(f32[344,8]{0,1:T(8,128)S(1)} %fusion.40), channel_id=1, replica_groups=mesh['dp'=4,'mp'=32] {'dp'}, use_global_device_ids=true, to_apply=%region_1.0 | all-reduce | flops 2752 | bytes 22016 | tf_op jit(solution)/shard_map/psum | solution.py:53
  43.3 0.6 slice_reduce_fusion.1
  43.9 65.1 %psum.120 = f32[]{:T(128)} all-reduce(f32[]{:T(128)} %get-tuple-element.11), channel_id=1, replica_groups=mesh['dp'=4,'mp'=32] {'mp'}, use_global_device_ids=true, to_apply=%region_3.0 | all-reduce | flops 1 | bytes 8 | tf_op jit(solution)/shard_map/psum | solution.py:20
  109.8 0.7 multiply_reduce_fusion
  110.4 63.2 %psum.121 = f32[]{:T(128)} all-reduce(f32[]{:T(128)} %multiply_reduce_fusion), channel_id=1, replica_groups=mesh['dp'=4,'mp'=32] {'mp'}, use_global_device_ids=true, to_apply=%region_4.0 | all-reduce | flops 1 | bytes 8 | tf_op jit(solution)/shard_map/psum | solution.py:18
  173.6 1.3 multiply_reduce_fusion.7
  174.9 63.2 %psum.122 = f32[]{:T(128)} all-reduce(f32[]{:T(128)} %multiply_reduce_fusion.7), channel_id=1, replica_groups=mesh['dp'=4,'mp'=32] {'mp'}, use_global_device_ids=true, to_apply=%region_6.0 | all-reduce | flops 1 | bytes 8 | tf_op jit(solution)/shard_map/psum | solution.py:20
  238.7 0.6 broadcast_multiply_fusion.7
  239.5 62.7 %psum.123 = f32[2]{0:T(128)S(1)} all-reduce(f32[2]{0:T(128)S(1)} %convolution_bitcast_fusion.2), channel_id=1, replica_groups=mesh['dp'=4,'mp'=32] {'mp'}, use_global_device_ids=true, to_apply=%region_7.0 | all-reduce | flops 2 | bytes 16 | tf_op jit(solution)/shard_map/psum | solution.py:18
  302.4 0.7 multiply_reduce_fusion.6
  303.0 63.2 %psum.124 = f32[]{:T(128)} all-reduce(f32[]{:T(128)} %get-tuple-element.24), channel_id=1, replica_groups=mesh['dp'=4,'mp'=32] {'mp'}, use_global_device_ids=true, to_apply=%region_9.0 | all-reduce | flops 1 | bytes 8 | tf_op jit(solution)/shard_map/psum | solution.py:20
  367.0 62.7 %psum.125 = f32[3]{0:T(128)S(1)} all-reduce(f32[3]{0:T(128)S(1)} %convolution_bitcast_fusion.1), channel_id=1, replica_groups=mesh['dp'=4,'mp'=32] {'mp'}, use_global_device_ids=true, to_apply=%region_10.0 | all-reduce | flops 3 | bytes 24 | tf_op jit(solution)/shard_map/psum | solution.py:18
  429.7 0.2 convolution_reduce_fusion.4
  429.9 1.3 multiply_reduce_fusion.5
  431.2 63.2 %psum.126 = f32[]{:T(128)} all-reduce(f32[]{:T(128)} %get-tuple-element.22), channel_id=1, replica_groups=mesh['dp'=4,'mp'=32] {'mp'}, use_global_device_ids=true, to_apply=%region_12.0 | all-reduce | flops 1 | bytes 8 | tf_op jit(solution)/shard_map/psum | solution.py:20
  495.2 63.2 %psum.127 = f32[4]{0:T(128)} all-reduce(f32[4]{0:T(128)S(1)} %convolution_bitcast_fusion), channel_id=1, replica_groups=mesh['dp'=4,'mp'=32] {'mp'}, use_global_device_ids=true, to_apply=%region_13.0 | all-reduce | flops 4 | bytes 32 | tf_op jit(solution)/shard_map/psum | solution.py:18
  558.3 0.8 convolution_reduce_fusion.3
  559.1 1.9 multiply_reduce_fusion.4
  561.0 63.2 %psum.128 = f32[]{:T(128)} all-reduce(f32[]{:T(128)} %get-tuple-element.20), channel_id=1, replica_groups=mesh['dp'=4,'mp'=32] {'mp'}, use_global_device_ids=true, to_apply=%region_15.0 | all-reduce | flops 1 | bytes 8 | tf_op jit(solution)/shard_map/psum | solution.py:20
  625.0 0.7 broadcast_multiply_fusion.4
  625.7 0.6 stack.34
  626.2 0.7 stack.35
  627.0 0.7 convolution_bitcast_fusion.5
  627.6 63.2 %psum.129 = f32[5]{0:T(128)} all-reduce(f32[5]{0:T(128)} %convolution_bitcast_fusion.5), channel_id=1, replica_groups=mesh['dp'=4,'mp'=32] {'mp'}, use_global_device_ids=true, to_apply=%region_16.0 | all-reduce | flops 5 | bytes 40 | tf_op jit(solution)/shard_map/psum | solution.py:18
  690.8 0.8 convolution_reduce_fusion.2
  691.5 1.3 multiply_reduce_fusion.3
  692.8 63.2 %psum.130 = f32[]{:T(128)} all-reduce(f32[]{:T(128)} %get-tuple-element.18), channel_id=1, replica_groups=mesh['dp'=4,'mp'=32] {'mp'}, use_global_device_ids=true, to_apply=%region_18.0 | all-reduce | flops 1 | bytes 8 | tf_op jit(solution)/shard_map/psum | solution.py:20
  756.7 0.6 stack.36
  757.2 0.7 stack.37
  757.9 0.7 convolution_bitcast_fusion.4
  758.6 63.2 %psum.131 = f32[6]{0:T(128)} all-reduce(f32[6]{0:T(128)} %convolution_bitcast_fusion.4), channel_id=1, replica_groups=mesh['dp'=4,'mp'=32] {'mp'}, use_global_device_ids=true, to_apply=%region_19.0 | all-reduce | flops 6 | bytes 48 | tf_op jit(solution)/shard_map/psum | solution.py:18
  821.8 0.8 convolution_reduce_fusion.1
  822.5 1.3 multiply_reduce_fusion.2
  823.8 63.2 %psum.132 = f32[]{:T(128)} all-reduce(f32[]{:T(128)} %get-tuple-element.16), channel_id=1, replica_groups=mesh['dp'=4,'mp'=32] {'mp'}, use_global_device_ids=true, to_apply=%region_21.0 | all-reduce | flops 1 | bytes 8 | tf_op jit(solution)/shard_map/psum | solution.py:20
  887.7 0.6 stack.38
  888.2 0.7 stack.39
  889.0 0.7 convolution_bitcast_fusion.3
  889.6 62.7 %psum.133 = f32[7]{0:T(128)S(1)} all-reduce(f32[7]{0:T(128)} %convolution_bitcast_fusion.3), channel_id=1, replica_groups=mesh['dp'=4,'mp'=32] {'mp'}, use_global_device_ids=true, to_apply=%region_22.0 | all-reduce | flops 7 | bytes 56 | tf_op jit(solution)/shard_map/psum | solution.py:18
  952.4 1.3 multiply_reduce_fusion.1
  953.7 63.2 %psum.134 = f32[]{:T(128)} all-reduce(f32[]{:T(128)} %get-tuple-element.14), channel_id=1, replica_groups=mesh['dp'=4,'mp'=32] {'mp'}, use_global_device_ids=true, to_apply=%region_24.0 | all-reduce | flops 1 | bytes 8 | tf_op jit(solution)/shard_map/psum | solution.py:20
  1017.6 0.7 stack.41
  1018.3 3.7 fusion.41
  1022.1 0.2 all-gather.2.cloned.1.call-start
  1022.3 136.1 %all-reduce.2.cloned.1.call-done = f32[4096,8]{0,1:T(8,128)} async-done(((f32[4096,8]{0,1:T(8,128)}), f32[4096,8]{0,1:T(8,128)}) %all-reduce.2.cloned.1.call-update) | async-done | bytes 131088 | tf_op jit(solution)/shard_map/psum | solution.py:55
  1158.4 5.6 fusion.5
  1164.0 2.4 copy-done.2
  1166.4 2.9 subtract_convert_fusion.1
  1169.4 4.8 fusion.37
  1174.2 2.6 fusion.1
  1176.8 6.0 convolution_add_fusion
  1182.8 6.7 fusion
  1189.5 14.1 %all-gather.2.cloned.1.call-done = bf16[344,4096]{1,0:T(8,128)(2,1)} async-done(((bf16[344,1024]{1,0:T(8,128)(2,1)}), bf16[344,4096]{1,0:T(8,128)(2,1)}) %all-gather.2.cloned.1.call-update) | async-done | bytes 2818064 | tf_op jit(solution)/shard_map/all_gather | solution.py:64
  1203.6 69.4 %reduce-scatter.2.cloned.1.call-done = f32[512,128]{1,0:T(8,128)} async-done(((f32[512,4096]{1,0:T(8,128)}), f32[512,128]{1,0:T(8,128)}) %reduce-scatter.2.cloned.1.call-update) | async-done | bytes 262160 | tf_op jit(solution)/shard_map/reduce_scatter | solution.py:49
  1273.0 1.6 convert_element_type.29
  1274.6 3.7 copy.16
  (43 shorter events, 1.0 us)
Async XLA Ops:
  8.0 1.8 copy-start
  8.0 1150.4 %all-reduce.2.cloned.1.call-start = ((), (), s32[]{:S(2)}) async-start(), calls=%async_computation.2 | async-start | bytes 262144 | tf_op jit(solution)/shard_map/psum | solution.py:55
  9.8 4.0 copy-start.7
  9.8 4.3 copy-start.13
  14.1 2.2 copy-start.3
  14.1 3.1 copy-start.4
  17.2 1.8 copy-start.5
  17.2 4.3 copy-start.10
  18.9 2.5 copy-start.1
  109.7 515.9 %copy-start.12 = (f32[344,1]{0,1:T(1,128)}, f32[344,1]{0,1:T(1,128)S(1)}, u32[]{:S(2)}) copy-start(f32[344,1]{0,1:T(1,128)S(1)} %get-tuple-element.27) | copy-start | bytes 4132
  495.0 130.6 %copy-start.11 = (f32[344,1]{0,1:T(1,128)}, f32[344,1]{0,1:T(1,128)S(1)}, u32[]{:S(2)}) copy-start(f32[344,1]{0,1:T(1,128)S(1)} %stack.32) | copy-start | bytes 4132
  1022.1 181.5 %all-gather.2.cloned.1.call-start = ((), (), s32[]{:S(2)}) async-start(), calls=%async_computation.3 | async-start | bytes 3522560 | tf_op jit(solution)/shard_map/all_gather | solution.py:64
  1158.4 8.0 copy-start.9
  1164.0 2.4 copy-start.2
  1169.3 103.7 %reduce-scatter.2.cloned.1.call-start = ((), (), s32[]{:S(2)}) async-start(), calls=%async_computation.1 | async-start | bytes 8650752 | tf_op jit(solution)/shard_map/reduce_scatter | solution.py:49
  1169.4 4.8 copy-start.6
  1174.2 2.6 copy-start.8
Sparse Core Ops, SparseCore 0:
  1022.2 136.1 all-reduce.1
  1169.4 34.1 all-gather.1
Sparse Core Ops, SparseCore 1:
  1182.9 90.1 reduce-scatter.1
where the time goes:
time: 1290 us
  blocking collectives  965 us (75%)
  waiting for transfers between devices  220 us (17%)
  matrix products  39.8 us (3%)
  other arithmetic  22.9 us (2%)
  between operations  21.1 us (2%)
  local copies, waits for them, and re-layouts  16.6 us (1%)
    psum x8, blocking collectives, orthonormal_split(): total = lax.psum(jnp.sum(vector * vector), 'mp')  507 us
    psum x7, blocking collectives, orthonormal_split(): coeffs = lax.psum(jnp.dot(basis.T, vector, precision=HIGH), 'mp')  441 us
    psum x1, waiting for transfers between devices, body(): right_down = lax.psum(contract_rows(m_down, left_down), ('dp', 'mp'))  136 us
    reduce_scatter x1, waiting for transfers between devices, body(): lax.psum_scatter(partial_sum, 'mp', scatter_dimension=1, tiled=True)  69.4 us
  transfers between devices with their start and end apart: 3, of which 3 were waited for; matrix products, arithmetic and copies ran while one was open for 2% of the time, Pallas kernels for 0%

commit v1 on v0

v1 whole, which is shorter than its diff:
```python
import functools

import jax
import jax.numpy as jnp
from jax import lax
from jax.experimental import pallas as pl
from jax.experimental.pallas import tpu as pltpu
from jax.sharding import PartitionSpec as P

MESH = pl.DeviceIdType.MESH
BF = jnp.bfloat16
F32 = jnp.float32
TOK, D, F, FP, R = 512, 4096, 344, 384, 8
KC = 1024
NK = D // KC
N_SEM = 128


def nt(a, b):
    return lax.dot_general(a, b, (((1,), (1,)), ((), ())), preferred_element_type=F32)


def nn(a, b):
    return lax.dot_general(a, b, (((1,), (0,)), ((), ())), preferred_element_type=F32)


def split3(v):
    hi = v.astype(BF).astype(F32)
    rest = v - hi
    mid = rest.astype(BF).astype(F32)
    low = rest - mid
    return jnp.concatenate([hi, mid, low, jnp.zeros_like(v)], axis=0).astype(BF)


def fold(r):
    return (r[0:8] + r[8:16]) + r[16:24]


def step_kernel(
    x_h, dy_h, wg_h, wu_h, wd_h, er_h, mo_h, q_h,
    ig_o, tg_o, m_o, sf_o, tt_o, pf_o,
    xs, dys, wgs, wus, wds, ers, mos, qs,
    wgp, wup, g, u, dh, hs, ht, dg, du, dgp, dup, ts, ms, q3,
    dyq, erq, pown, py_r, p3, pg, ct,
    sb, sc_r, sx_r, s1, sz_r, s2, sy_r, sf, tt, pf,
    rs_p, ra_r, rb_r, a1, b1, za_r, xb_r, igs,
    load_sem, send_sem, recv_sem,
):
    dp = lax.axis_index("dp")
    mp = lax.axis_index("mp")
    core = lax.rem(mp, 2)
    z = lax.rem(mp // 2, 4)
    x = mp // 8
    other = 1 - core

    def wrap(v):
        return lax.rem(v, 4)

    to_core = (dp, mp + 1 - 2 * core)

    def to_x(d):
        return (dp, wrap(x + d) * 8 + z * 2 + core)

    def to_z(d):
        return (dp, x * 8 + wrap(z + d) * 2 + core)

    def to_y(d):
        return (wrap(dp + d), mp)

    barrier = pltpu.get_barrier_semaphore()
    peers = [to_core] + [f(d) for f in (to_x, to_z, to_y) for d in (1, 2, 3)]
    for peer in peers:
        pl.semaphore_signal(barrier, inc=1, device_id=peer, device_id_type=MESH)

    def lx(k):
        return pltpu.make_async_copy(x_h.at[:, pl.ds(k * KC, KC)], xs.at[k], load_sem.at[k])

    def ly(k):
        return pltpu.make_async_copy(dy_h.at[:, pl.ds(k * KC, KC)], dys.at[k], load_sem.at[4 + k])

    def lwd(k):
        return pltpu.make_async_copy(wd_h.at[:, pl.ds(k * KC, KC)], wds.at[k], load_sem.at[8 + k])

    def ler(k):
        return pltpu.make_async_copy(er_h.at[:, pl.ds(k * KC, KC)], ers.at[k], load_sem.at[12 + k])

    def lwg(b):
        return pltpu.make_async_copy(
            wg_h.at[:, pl.ds(b * 128, 128)], wgs.at[b // 2, b % 2], load_sem.at[18 + b]
        )

    def lwu(b):
        return pltpu.make_async_copy(
            wu_h.at[:, pl.ds(b * 128, 128)], wus.at[b // 2, b % 2], load_sem.at[50 + b]
        )

    lmo = pltpu.make_async_copy(mo_h, mos, load_sem.at[16])
    lq = pltpu.make_async_copy(q_h, qs, load_sem.at[17])
    for k in range(NK):
        lx(k).start()
        for b in range(8):
            lwg(8 * k + b).start()
            lwu(8 * k + b).start()
    lq.start()
    lmo.start()
    for k in range(NK):
        lwd(k).start()
    for k in range(NK):
        ly(k).start()
    for k in range(NK):
        ler(k).start()

    count = [0]
    sent = []

    def send(src, dst, device):
        i = count[0]
        count[0] += 1
        c = pltpu.make_async_remote_copy(
            src_ref=src, dst_ref=dst, send_sem=send_sem.at[i], recv_sem=recv_sem.at[i],
            device_id=device, device_id_type=MESH,
        )
        c.start()
        sent.append(c)
        return c

    g[...] = jnp.zeros_like(g)
    u[...] = jnp.zeros_like(u)
    dh[...] = jnp.zeros_like(dh)
    dyq[...] = jnp.zeros_like(dyq)
    erq[...] = jnp.zeros_like(erq)
    hs[...] = jnp.zeros_like(hs)
    pown[...] = jnp.zeros_like(pown)
    pf[...] = jnp.zeros_like(pf)

    @pl.loop(0, NK)
    def _(k):
        lx(k).wait()
        for b in range(8):
            lwg(8 * k + b).wait()
            lwu(8 * k + b).wait()
        a = xs[k]
        wg = jnp.concatenate([wgs[4 * k + b // 2, b % 2] for b in range(8)], axis=1)
        g[...] += nt(a, wg)
        wu = jnp.concatenate([wus[4 * k + b // 2, b % 2] for b in range(8)], axis=1)
        u[...] += nt(a, wu)

    pl.semaphore_wait(barrier, len(peers))
    send_wg = send(wgs.at[:, other], wgp, to_core)
    send_wu = send(wus.at[:, other], wup, to_core)

    lmo.wait()
    for k in range(NK):
        lwd(k).wait()
    for p in range(8):
        lanes = pl.ds(p * 128, 128)
        ts[p] = (wds[dp, :, lanes].astype(F32) - 0.1 * (0.9 * mos[:, lanes])).astype(BF)
    own_t = pltpu.make_async_copy(ts, tg_o.at[dp], load_sem.at[82])
    own_t.start()
    right, left = wrap(dp + 1), wrap(dp + 3)
    t_right, t_left, t_far = [], [], []

    def t_slot(s):
        if s < 8:
            t_right.append(send(ts.at[s], tg_o.at[dp, s], to_y(1)))
            t_left.append(send(ts.at[s], tg_o.at[dp, s], to_y(3)))
        if 1 <= s <= 8:
            p = s - 1
            if p % 2 == 0:
                t_right[p].wait_recv()
                t_far.append(send(tg_o.at[left, p], tg_o.at[left, p], to_y(1)))
            else:
                t_left[p].wait_recv()
                t_far.append(send(tg_o.at[right, p], tg_o.at[right, p], to_y(3)))

    t_slot(0)

    lq.wait()
    for k in range(NK):
        q3[k] = split3(qs[:, k * KC : (k + 1) * KC])

    @pl.loop(0, NK)
    def _(k):
        ly(k).wait()
        dh[...] += nt(dys[k], wds[k])
        dyq[...] += nt(q3[k], dys[k])

    @pl.loop(0, NK)
    def _(k):
        ler(k).wait()
        erq[...] += nt(q3[k], ers[k])

    @pl.loop(0, 8)
    def _(i):
        rows = pl.ds(pl.multiple_of(i * 64, 64), 64)
        gv, uv, dv = g[rows, :], u[rows, :], dh[rows, :]
        sig = jax.nn.sigmoid(gv)
        gs = gv * sig
        hs[rows, 0:F] = (gs * uv).astype(BF)
        dg[rows, :] = (dv * uv * sig * (1.0 + gv * (1.0 - sig))).astype(BF)
        du[rows, :] = (dv * gs).astype(BF)

    send_dg = send(dg, dgp, to_core)
    send_du = send(du, dup, to_core)

    pown[:, 0:F] = fold(nn(split3(fold(dyq[...])), hs[:, 0:F])) + fold(erq[...])
    c_py = [send(pown, py_r.at[d - 1], to_y(d)) for d in (1, 2, 3)]
    t_slot(1)

    ht[...] = hs[...].astype(F32).T.astype(BF)

    @pl.loop(0, NK)
    def _(k):
        ms[k] = nn(ht[0:F, :], dys[k]) + ers[k].astype(F32)
        pltpu.make_async_copy(ms.at[k], m_o.at[k], load_sem.at[83 + k]).start()

    for c in c_py:
        c.wait_recv()
    pf[...] = ((pown[...] + py_r[1]) + (py_r[0] + py_r[2])) * 0.25
    base = z * 24 + x * 6 + core * 3
    for c in range(3):
        pg[base + c] = pf[:, c * 128 : (c + 1) * 128]
    c_pgc = send(pg.at[pl.ds(base, 3)], pg.at[pl.ds(base, 3)], to_core)

    p3[...] = split3(pf[...])
    hp3 = split3(fold(nt(p3[...], hs[...])))

    def s_part(c):
        s = fold(nn(hp3, dys[c]) + nn(p3[:, 0:F], ers[c]))
        for j in range(8):
            sb[8 * c + j] = s[:, j * 128 : (j + 1) * 128]

    s_part(2 * other)
    s_part(2 * other + 1)
    c_sc = send(sb.at[pl.ds(16 * other, 16)], sc_r, to_core)
    s_part(2 * core)
    s_part(2 * core + 1)

    c_pgc.wait_recv()
    xy = z * 24 + x * 6
    c_pgx = [send(pg.at[pl.ds(xy, 6)], pg.at[pl.ds(xy, 6)], to_x(d)) for d in (1, 2, 3)]
    c_sc.wait_recv()
    half = pl.ds(16 * core, 16)
    sb[half] = sb[half] + sc_r[...]
    c_sx = [
        send(sb.at[pl.ds(16 * core + 4 * wrap(x + d), 4)], sx_r.at[d - 1], to_x(d))
        for d in (1, 2, 3)
    ]
    t_slot(2)

    send_wg.wait_recv()
    send_wu.wait_recv()
    send_dg.wait_recv()
    send_du.wait_recv()

    @pl.loop(0, 8)
    def _(i):
        a, b = 2 * i, 2 * i + 1
        r = nn(dg[...], jnp.concatenate([wgs[a, core], wgs[b, core]], axis=1))
        r += nn(du[...], jnp.concatenate([wus[a, core], wus[b, core]], axis=1))
        r += nn(dgp[...], jnp.concatenate([wgp[a], wgp[b]], axis=1))
        r += nn(dup[...], jnp.concatenate([wup[a], wup[b]], axis=1))
        rs_p[a] = r[:, 0:128].astype(BF)
        rs_p[b] = r[:, 128:256].astype(BF)

    top, bottom = pl.ds(0, 256), pl.ds(256, 256)
    c_a, c_b = {}, {}

    def bulk(j):
        for d in (1, 3, 2):
            c_a[j, d] = send(
                rs_p.at[wrap(x + d) * 4 + wrap(z + j), top], ra_r.at[d - 1, j], to_x(d)
            )
            c_b[j, d] = send(
                rs_p.at[wrap(x + j) * 4 + wrap(z + d), bottom], rb_r.at[d - 1, j], to_z(d)
            )

    for c in c_sx:
        c.wait_recv()
    s1[...] = (sb[pl.ds(16 * core + 4 * x, 4)] + sx_r[0]) + (sx_r[1] + sx_r[2])
    c_sz = [send(s1.at[wrap(z + d)], sz_r.at[d - 1], to_z(d)) for d in (1, 2, 3)]
    for c in c_pgx:
        c.wait_recv()
    zz = z * 24
    c_pgz = [send(pg.at[pl.ds(zz, 24)], pg.at[pl.ds(zz, 24)], to_z(d)) for d in (1, 2, 3)]
    bulk(1)
    for c in c_sz:
        c.wait_recv()
    s2[...] = (s1[z] + sz_r[0]) + (sz_r[1] + sz_r[2])
    c_sy = [send(s2, sy_r.at[d - 1], to_y(d)) for d in (1, 2, 3)]
    t_slot(3)
    bulk(2)

    for c in c_pgz:
        c.wait_recv()
    for i in range(12):
        ct[:, i] = jnp.transpose(pg[8 * i : 8 * i + 8], (1, 0, 2))
    lane = lax.broadcasted_iota(jnp.int32, (1, 128), 1)
    done_b, done_t = [], []

    def total(v):
        v = jnp.sum(v, axis=0)
        return jnp.sum(jnp.sum(v, axis=0, keepdims=True), axis=1, keepdims=True)

    for k in range(R):
        v = ct[k]
        t = jnp.where(lane == k, 1.0, 0.0)
        coeffs = [total(b * v) for b in done_b]
        for c, b, tb in zip(coeffs, done_b, done_t):
            v = v - c[None] * b
            t = t - c * tb
        scale = lax.rsqrt(total(v * v) + 1e-06)
        done_b.append(v * scale[None])
        done_t.append(t * scale)
        tt[k : k + 1, :] = done_t[-1]

    for c in c_sy:
        c.wait_recv()
    mine = core * 16 + x * 4 + z
    sf[mine] = (s2[...] + sy_r[1]) + (sy_r[0] + sy_r[2])
    c_gz = [send(sf.at[mine], sf.at[mine], to_z(d)) for d in (1, 2, 3)]
    t_slot(4)
    bulk(3)
    for c in c_gz:
        c.wait_recv()
    mx = pl.ds(core * 16 + x * 4, 4)
    c_gx = [send(sf.at[mx], sf.at[mx], to_x(d)) for d in (1, 2, 3)]
    t_slot(5)
    bulk(0)
    for c in c_gx:
        c.wait_recv()
    mc = pl.ds(core * 16, 16)
    c_gc = send(sf.at[mc], sf.at[mc], to_core)

    def first_sums(j):
        for d in (1, 2, 3):
            c_a[j, d].wait_recv()
            c_b[j, d].wait_recv()
        a = rs_p[x * 4 + wrap(z + j), top, :].astype(F32)
        a = (a + ra_r[0, j].astype(F32)) + (ra_r[1, j].astype(F32) + ra_r[2, j].astype(F32))
        b = rs_p[wrap(x + j) * 4 + z, bottom, :].astype(F32)
        b = (b + rb_r[0, j].astype(F32)) + (rb_r[1, j].astype(F32) + rb_r[2, j].astype(F32))
        return a, b

    c_za, c_xb = [], []
    for j in (1, 2, 3):
        t_slot(5 + j)
        a, b = first_sums(j)
        a1[j] = a.astype(BF)
        b1[j] = b.astype(BF)
        c_za.append(send(a1.at[j], za_r.at[j - 1], to_z(j)))
        c_xb.append(send(b1.at[j], xb_r.at[j - 1], to_x(j)))
    a, b = first_sums(0)
    for c in c_za:
        c.wait_recv()
    igs[0:256, :] = (
        (a + za_r[0].astype(F32)) + (za_r[1].astype(F32) + za_r[2].astype(F32))
    ).astype(BF)
    for c in c_xb:
        c.wait_recv()
    igs[256:512, :] = (
        (b + xb_r[0].astype(F32)) + (xb_r[1].astype(F32) + xb_r[2].astype(F32))
    ).astype(BF)

    c_gc.wait_recv()
    outs = [
        pltpu.make_async_copy(igs, ig_o, load_sem.at[87]),
        pltpu.make_async_copy(sf, sf_o, load_sem.at[88]),
        pltpu.make_async_copy(tt, tt_o, load_sem.at[89]),
        pltpu.make_async_copy(pf, pf_o, load_sem.at[90]),
    ]
    for c in outs:
        c.start()
    for p in range(8):
        if p % 2 == 0:
            t_left[p].wait_recv()
        else:
            t_right[p].wait_recv()
    for c in t_far:
        c.wait_recv()
    for c in sent:
        c.wait_send()
    for c in outs:
        c.wait()
    own_t.wait()
    for k in range(NK):
        pltpu.make_async_copy(ms.at[k], m_o.at[k], load_sem.at[83 + k]).wait()


def exchange(x, dy, wg, wu, wd, er, mo, q):
    v = pltpu.VMEM
    any_spec = pl.BlockSpec(memory_space=pl.ANY)
    scratch = [
        v((NK, TOK, KC), BF), v((NK, TOK, KC), BF),
        v((16, 2, F, 128), BF), v((16, 2, F, 128), BF),
        v((NK, F, KC), BF), v((NK, F, KC), BF), v((F, KC), F32), v((R, D), F32),
        v((16, F, 128), BF), v((16, F, 128), BF),
        v((TOK, F), F32), v((TOK, F), F32), v((TOK, F), F32),
        v((TOK, FP), BF), v((FP, TOK), BF),
        v((TOK, F), BF), v((TOK, F), BF), v((TOK, F), BF), v((TOK, F), BF),
        v((8, F, 128), BF), v((NK, F, KC), F32), v((NK, 32, KC), BF),
        v((32, TOK), F32), v((32, F), F32), v((R, FP), F32), v((3, R, FP), F32),
        v((32, FP), BF), v((96, 8, 128), F32), v((8, 12, 8, 128), F32),
        v((32, 8, 128), F32), v((16, 8, 128), F32), v((3, 4, 8, 128), F32),
        v((4, 8, 128), F32), v((3, 8, 128), F32), v((8, 128), F32), v((3, 8, 128), F32),
        v((32, 8, 128), F32), v((8, 128), F32), v((R, FP), F32),
        v((16, TOK, 128), BF), v((3, 4, 256, 128), BF), v((3, 4, 256, 128), BF),
        v((4, 256, 128), BF), v((4, 256, 128), BF), v((3, 256, 128), BF), v((3, 256, 128), BF),
        v((TOK, 128), BF),
        pltpu.SemaphoreType.DMA((96,)),
        pltpu.SemaphoreType.DMA((N_SEM,)),
        pltpu.SemaphoreType.DMA((N_SEM,)),
    ]
    out_shape = (
        jax.ShapeDtypeStruct((TOK, 128), BF),
        jax.ShapeDtypeStruct((4, 8, F, 128), BF),
        jax.ShapeDtypeStruct((NK, F, KC), F32),
        jax.ShapeDtypeStruct((32, 8, 128), F32),
        jax.ShapeDtypeStruct((8, 128), F32),
        jax.ShapeDtypeStruct((R, FP), F32),
    )
    return pl.pallas_call(
        step_kernel,
        out_shape=out_shape,
        in_specs=[any_spec] * 8,
        out_specs=[any_spec] * 6,
        scratch_shapes=scratch,
        compiler_params=pltpu.CompilerParams(
            collective_id=0, has_side_effects=True, vmem_limit_bytes=62 * 1024 * 1024
        ),
        name="exchange",
    )(x, dy, wg, wu, wd, er, mo, q)


def apply_kernel(ig_ref, t_ref, m_ref, mo_ref, sf_ref, tt_ref, pf_ref,
                 igo_ref, nd_ref, ne_ref, nm_ref, left):
    j = pl.program_id(0)
    dp = lax.axis_index("dp")

    @pl.when(j == 0)
    def _():
        igo_ref[...] = ig_ref[...]
        p = jnp.zeros((R, FP), F32)
        for i in range(R):
            p += tt_ref[:, i : i + 1] * pf_ref[i : i + 1, :]
        hi = p.astype(BF).astype(F32)
        rest = p - hi
        mid = rest.astype(BF).astype(F32)
        low = rest - mid
        rows = [hi, hi, mid, hi, low, mid] + [jnp.zeros_like(p)] * 10
        left[...] = jnp.concatenate(rows, axis=0).T.astype(BF)

    def q_rows(s):
        q = jnp.zeros((R, 128), F32)
        for i in range(R):
            q += tt_ref[:, i : i + 1] * s[i : i + 1, :]
        q = q * 0.25
        hi = q.astype(BF).astype(F32)
        rest = q - hi
        mid = rest.astype(BF).astype(F32)
        low = rest - mid
        rows = [hi, mid, hi, low, hi, mid] + [jnp.zeros_like(q)] * 10
        return jnp.concatenate(rows, axis=0).astype(BF)

    right = jnp.concatenate([q_rows(sf_ref[4 * j + c]) for c in range(4)], axis=1)
    approx = nn(left[0:F, :], right)
    ne_ref[...] = (m_ref[0] - approx).astype(BF)
    for c in range(4):
        lanes = slice(c * 128, (c + 1) * 128)
        nd_ref[:, lanes] = (t_ref[0, c].astype(F32) - 0.1 * approx[:, lanes]).astype(BF)
    nm_ref[...] = 0.9 * mo_ref[...] + nn(left[0:F, :], q_rows(sf_ref[dp * 8 + j]))


def apply(ig, tg, m, mo, sf, tt, pf):
    def whole(a):
        return pl.BlockSpec(a.shape, lambda j: (0,) * a.ndim)

    return pl.pallas_call(
        apply_kernel,
        grid=(8,),
        out_shape=(
            jax.ShapeDtypeStruct((TOK, 128), BF),
            jax.ShapeDtypeStruct((F, D), BF),
            jax.ShapeDtypeStruct((F, D), BF),
            jax.ShapeDtypeStruct((F, KC), F32),
        ),
        in_specs=[
            whole(ig),
            pl.BlockSpec((1, 4, F, 128), lambda j: (j // 2, j % 2, 0, 0)),
            pl.BlockSpec((1, F, 512), lambda j: (j // 2, 0, j % 2)),
            pl.BlockSpec((F, 128), lambda j: (0, j)),
            whole(sf), whole(tt), whole(pf),
        ],
        out_specs=[
            pl.BlockSpec((TOK, 128), lambda j: (0, 0)),
            pl.BlockSpec((F, 512), lambda j: (0, j)),
            pl.BlockSpec((F, 512), lambda j: (0, j)),
            pl.BlockSpec((F, 128), lambda j: (0, j)),
        ],
        scratch_shapes=[pltpu.VMEM((FP, 128), BF)],
        name="apply",
    )(ig, tg, m, mo, sf, tt, pf)


def body(inputs, out_grads, w_gate, w_up, w_down, err_down, mom_down, q_down):
    ig, tg, m, sf, tt, pf = exchange(
        inputs, out_grads, w_gate.T, w_up.T, w_down, err_down[0], mom_down, q_down.T
    )
    ig, nd, ne, nm = apply(ig, tg, m, mom_down, sf, tt, pf)
    return ig, nd, ne[None], nm


def solution(mesh):
    in_specs = (
        P("dp", None), P("dp", None), P(None, "mp"), P(None, "mp"), P("mp", None),
        P("dp", "mp", None), P("mp", "dp"), P(),
    )
    out_specs = (P("dp", "mp"), P("mp", None), P("dp", "mp", None), P("mp", "dp"))
    return jax.shard_map(body, mesh=mesh, in_specs=in_specs, out_specs=out_specs, check_vma=False)
```

time: 1290 us -> 70.9 us (0.05)
  blocking collectives: 965 us -> 0 us
  waiting for transfers between devices: 220 us -> 0 us
  Pallas kernels: 0 us -> 69.8 us
  matrix products: 39.8 us -> 0 us
  other arithmetic: 22.9 us -> 0 us
  between operations: 21.1 us -> 0.64 us
  local copies, waits for them, and re-layouts: 16.6 us -> 0 us
    psum x16 -> x0, blocking collectives: 965 us -> none  [the longest x8 507 us: orthonormal_split(): total = lax.psum(jnp.sum(vector * vector), 'mp')]
    psum x1 -> x0, waiting for transfers between devices: 136 us -> none  [body(): right_down = lax.psum(contract_rows(m_down, left_down), ('dp', 'mp'))]
    pallas_call x0 -> x2, Pallas kernels: none -> 69.8 us  [the longest x1 59.5 us: exchange(): pl.pallas_call(step_kernel, out_shape=out_shape, in_specs=[any_spec] * 8,...]
    reduce_scatter x1 -> x0, waiting for transfers between devices: 69.4 us -> none  [body(): lax.psum_scatter(partial_sum, 'mp', scatter_dimension=1, tiled=True)]
    dot_general x21 -> x0, matrix products: 39.8 us -> none  [the longest x3 13.3 us: contract_cols(): lax.dot_general(left, right, (((1,), (1,)), ((), ())), preferred_element_...]
    all_gather x1 -> x0, waiting for transfers between devices: 14.1 us -> none  [body(): new_down = lax.all_gather(own_down, 'dp', axis=1, tiled=True)]
  transfers between devices with their start and end apart: 3 -> 0, of which waited for: 3 -> 0; matrix products, arithmetic and copies ran while one was open for 2% -> 0% of each run, Pallas kernels for 0% -> 0%
where the time goes in v1:
time: 70.9 us; the launch traced here: 70.4 us
  Pallas kernels  69.8 us (98%)
    pallas_call x1, Pallas kernels, exchange(): pl.pallas_call(step_kernel, out_shape=out_shape, in_specs=[any_spec] * 8,...  59.5 us
    pallas_call x1, Pallas kernels, apply(): pl.pallas_call(apply_kernel, grid=(8,), out_shape=(jax.ShapeDtypeStruct((...  10.2 us

profile of v1, /device:TPU:0, one launch (start us, length us, event | category | flops | bytes accessed | tf_op | source)
XLA Modules:
  0.0 70.4 jit_solution(4053962741254795546)
XLA Ops:
  0.6 59.5 %exchange.1 = (bf16[512,128]{1,0:T(8,128)(2,1)}, bf16[4,8,344,128]{3,2,1,0:T(8,128)(2,1)}, f32[4,344,1024]{2,1,0:T(8,128)}, f32[32,8,128]{2,1,0:T(8,128)}, f32[8,128]{1,0:T(8,128)}, /*index=5*/f32[8,384]{1,0:T(8,128)}) custom-call(bf16[512,4096]{1,0:T(8,128)(2,1)} %x_h.1, bf16[512,4096]{1,0:T(8,128)(2,1)} %dy_h.1, bf16[344,4096]{1,0:T(8,128)(2,1)} %bitcast.5, ...), custom_call_target="tpu_custom_call" | custom-call | tf_op jit(solution)/shard_map/exchange/pallas_call | solution.py:422
  60.2 10.2 %apply.1 = (bf16[512,128]{1,0:T(8,128)(2,1)}, bf16[344,4096]{1,0:T(8,128)(2,1)}, bf16[344,4096]{1,0:T(8,128)(2,1)}, f32[344,1024]{1,0:T(8,128)}) custom-call(bf16[512,128]{1,0:T(8,128)(2,1)} %get-tuple-element.14.ig_ref, bf16[4,8,344,128]{3,2,1,0:T(8,128)(2,1)} %get-tuple-element.15.t_ref, f32[4,344,1024]{2,1,0:T(8,128)} %get-tuple-element.16.m_ref, ...), custom_call_target="tpu_custom_call" | custom-call | tf_op jit(solution)/shard_map/apply/pallas_call | solution.py:478

commit v2 on v1

v2 whole, which is shorter than its diff:
```python
import jax
import jax.numpy as jnp
from jax import lax
from jax.experimental import pallas as pl
from jax.experimental.pallas import tpu as pltpu
from jax.sharding import PartitionSpec as P

MESH = pl.DeviceIdType.MESH
BF = jnp.bfloat16
F32 = jnp.float32
TOK, D, F, FP, R = 512, 4096, 344, 384, 8
UP = 352
KP = 768
KC = 1024
NK = D // KC
N_SEM = 112


def nt(a, b):
    return lax.dot_general(a, b, (((1,), (1,)), ((), ())), preferred_element_type=F32)


def nn(a, b):
    return lax.dot_general(a, b, (((1,), (0,)), ((), ())), preferred_element_type=F32)


def parts(v):
    hi = v.astype(BF).astype(F32)
    rest = v - hi
    mid = rest.astype(BF).astype(F32)
    return hi, mid, rest - mid


def split3(v):
    hi, mid, low = parts(v)
    return jnp.concatenate([hi, mid, low, jnp.zeros_like(v)], axis=0).astype(BF)


def fold(r):
    return (r[0:8] + r[8:16]) + r[16:24]


def wrap(v):
    return lax.rem(v, 4)


def step_kernel(
    x_h, dy_h, wg_h, wu_h, wd_h, er_h, mo_h, q_h,
    igs, tg, ms, mos, left, right,
    xs, dys, ws, wds, ers, qs, wsp,
    gu, dhq, ht, dt, dc, dcp, erq,
    pown, py_r, p3, pf, pg, ct, tt,
    sb, sc_r, sx_r, s1, sz_r, s2, sy_r, sf,
    rsf, rsp, hap, ham, hbp, hbm, rap, ram, rbp, rbm, a1, b1, za_r, xb_r,
    load_sem, send_sem, recv_sem,
):
    dp = lax.axis_index("dp")
    mp = lax.axis_index("mp")
    core = lax.rem(mp, 2)
    z = lax.rem(mp // 2, 4)
    x = mp // 8
    other = 1 - core
    to_core = (dp, mp + 1 - 2 * core)

    def to_x(d):
        return (dp, wrap(x + d) * 8 + z * 2 + core)

    def to_z(d):
        return (dp, x * 8 + wrap(z + d) * 2 + core)

    def to_y(d):
        return (wrap(dp + d), mp)

    barrier = pltpu.get_barrier_semaphore()
    peers = [to_core] + [f(d) for f in (to_x, to_z, to_y) for d in (1, 2, 3)]
    for peer in peers:
        pl.semaphore_signal(barrier, inc=1, device_id=peer, device_id_type=MESH)

    def lx(k):
        cols = pl.ds(k * 512, 512)
        return pltpu.make_async_copy(x_h.at[:, cols], xs.at[k], load_sem.at[k])

    def lwg(b):
        return pltpu.make_async_copy(
            wg_h.at[:, pl.ds(b * 128, 128)], ws.at[b // 2, b % 2, pl.ds(0, F)], load_sem.at[8 + b]
        )

    def lwu(b):
        return pltpu.make_async_copy(
            wu_h.at[:, pl.ds(b * 128, 128)], ws.at[b // 2, b % 2, pl.ds(UP, F)], load_sem.at[40 + b]
        )

    def ly(k):
        return pltpu.make_async_copy(dy_h.at[:, pl.ds(k * KC, KC)], dys.at[k], load_sem.at[72 + k])

    def lwd(k):
        return pltpu.make_async_copy(
            wd_h.at[:, pl.ds(k * KC, KC)], wds.at[k, pl.ds(0, F)], load_sem.at[76 + k]
        )

    def ler(k):
        return pltpu.make_async_copy(er_h.at[:, pl.ds(k * KC, KC)], ers.at[k], load_sem.at[80 + k])

    lmo = pltpu.make_async_copy(mo_h, mos, load_sem.at[84])
    lq = pltpu.make_async_copy(q_h, qs, load_sem.at[85])
    for k in range(8):
        lx(k).start()
        for b in range(4):
            lwg(4 * k + b).start()
            lwu(4 * k + b).start()
        if k == 1:
            lmo.start()
            lwd(dp).start()
    lq.start()
    ly(dp).start()
    for i in range(1, NK):
        ly(wrap(dp + i)).start()
        lwd(wrap(dp + i)).start()
    for k in range(NK):
        ler(k).start()

    count = [0]
    sent = []

    def send(src, dst, device):
        i = count[0]
        count[0] += 1
        c = pltpu.make_async_remote_copy(
            src_ref=src, dst_ref=dst, send_sem=send_sem.at[i], recv_sem=recv_sem.at[i],
            device_id=device, device_id_type=MESH,
        )
        c.start()
        sent.append(c)
        return c

    for ref in (gu, dhq, erq, pown):
        ref[...] = jnp.zeros_like(ref)
    ws[:, :, F:UP, :] = jnp.zeros((16, 2, UP - F, 128), BF)
    ws[:, :, UP + F :, :] = jnp.zeros((16, 2, KP - UP - F, 128), BF)
    wds[:, F:UP, :] = jnp.zeros((NK, UP - F, KC), BF)
    dt[F:UP, :] = jnp.zeros((UP - F, TOK), dt.dtype)
    dt[UP + F :, :] = jnp.zeros((KP - UP - F, TOK), dt.dtype)

    def gate_up(k):
        lx(k).wait()
        for b in range(4):
            lwg(4 * k + b).wait()
            lwu(4 * k + b).wait()
        w = jnp.concatenate([ws[2 * k + b // 2, b % 2, 0:704] for b in range(4)], axis=1)
        gu[...] += nt(w, xs[k])

    pl.loop(0, 2)(gate_up)

    pl.semaphore_wait(barrier, len(peers))
    lmo.wait()
    lwd(dp).wait()
    for p in range(8):
        lanes = pl.ds(p * 128, 128)
        tg[dp, p] = (wds[dp, 0:F, lanes].astype(F32) - 0.1 * (0.9 * mos[:, lanes])).astype(BF)
    y_right, y_left = wrap(dp + 1), wrap(dp + 3)
    t_right, t_left, t_far = {}, {}, []

    def t_own(*pieces):
        for p in pieces:
            t_right[p] = send(tg.at[dp, p], tg.at[dp, p], to_y(1))
            t_left[p] = send(tg.at[dp, p], tg.at[dp, p], to_y(3))

    def t_on(*pieces):
        for p in pieces:
            if p % 2 == 0:
                t_right[p].wait_recv()
                t_far.append(send(tg.at[y_left, p], tg.at[y_left, p], to_y(1)))
            else:
                t_left[p].wait_recv()
                t_far.append(send(tg.at[y_right, p], tg.at[y_right, p], to_y(3)))

    t_own(0, 1, 2)

    pl.loop(2, 8)(gate_up)
    c_w = send(ws.at[:, other], wsp, to_core)

    lq.wait()
    for k in range(NK):
        wds[k, UP:FP, :] = split3(qs[:, k * KC : (k + 1) * KC])

    @pl.loop(0, NK)
    def _(i):
        k = wrap(dp + i)
        ly(k).wait()

        @pl.when(i > 0)
        def _():
            lwd(k).wait()

        dhq[...] += nt(wds[k], dys[k])

    @pl.loop(0, NK)
    def _(k):
        ler(k).wait()
        erq[0:F, 0:32] += nt(ers[k], wds[k, UP:FP, :])

    @pl.loop(0, 4)
    def _(i):
        lanes = pl.ds(pl.multiple_of(i * 128, 128), 128)
        gv, uv, dv = gu[0:F, lanes], gu[UP : UP + F, lanes], dhq[0:F, lanes]
        sig = jax.nn.sigmoid(gv)
        gs = gv * sig
        ht[:, lanes] = (gs * uv).astype(BF)
        dt[0:F, lanes] = (dv * uv * sig * (1.0 + gv * (1.0 - sig))).astype(dt.dtype)
        dt[UP : UP + F, lanes] = (dv * gs).astype(dt.dtype)

    own_p = fold(nt(split3(fold(dhq[UP:FP, :])), ht[...]))
    pown[:, 0:F] = own_p + fold(erq[...].T[0:32, 0:F])
    c_py = [send(pown, py_r.at[d - 1], to_y(d)) for d in (1, 3, 2)]

    t_on(0, 1, 2)
    t_own(3)
    dc[...] = dt[...].T.astype(BF)
    c_dc = send(dc, dcp, to_core)

    @pl.loop(0, 8)
    def _(i):
        a = 2 * i
        r = nn(dc[...], jnp.concatenate([ws[a, core], ws[a + 1, core]], axis=1))
        rsf[i // 2, 2 * lax.rem(i, 2)] = r[:, 0:128]
        rsf[i // 2, 2 * lax.rem(i, 2) + 1] = r[:, 128:256]

    for c in c_py:
        c.wait_recv()
    pf[...] = ((pown[...] + py_r[1]) + (py_r[0] + py_r[2])) * 0.25
    base = core * 48 + z * 12
    for c in range(3):
        pg[base + x * 3 + c] = pf[:, c * 128 : (c + 1) * 128]
    own = pl.ds(base + x * 3, 3)
    c_pgx = [send(pg.at[own], pg.at[own], to_x(d)) for d in (1, 3, 2)]
    p3[...] = split3(pf[...])
    hp3 = split3(fold(nn(p3[:, 0:F], ht[...])))

    def s_part(c):
        s = fold(nn(hp3, dys[c]) + nn(p3[:, 0:F], ers[c]))
        for j in range(8):
            sb[8 * c + j] = s[:, j * 128 : (j + 1) * 128]

    s_part(2 * other)
    s_part(2 * other + 1)
    c_sc = send(sb.at[pl.ds(16 * other, 16)], sc_r, to_core)
    s_part(2 * core)
    s_part(2 * core + 1)
    t_on(3)
    t_own(4)

    c_w.wait_recv()
    c_dc.wait_recv()

    def rs_peer(i):
        a = 2 * i
        r = nn(dcp[...], jnp.concatenate([wsp[a], wsp[a + 1]], axis=1))
        for n in range(2):
            at = (i // 2, 2 * lax.rem(i, 2) + n)
            v = rsf[at] + r[:, n * 128 : (n + 1) * 128]
            rsf[at] = v
            rsp[at] = v.astype(BF)

    pl.loop(0, 3)(rs_peer)
    c_sc.wait_recv()
    half = pl.ds(16 * core, 16)
    sb[half] = sb[half] + sc_r[...]
    c_sx = [
        send(sb.at[pl.ds(16 * core + 4 * wrap(x + d), 4)], sx_r.at[d - 1], to_x(d))
        for d in (1, 3, 2)
    ]
    t_on(4)
    t_own(5)
    pl.loop(3, 8)(rs_peer)
    for c in c_pgx:
        c.wait_recv()
    own = pl.ds(base, 12)
    c_pgz = [send(pg.at[own], pg.at[own], to_z(d)) for d in (1, 3, 2)]
    x1, x2, x3 = wrap(x + 1), wrap(x + 2), wrap(x + 3)
    z1, z2, z3 = wrap(z + 1), wrap(z + 2), wrap(z + 3)
    q0, q1, q2, q3 = (pl.ds(n * 128, 128) for n in range(4))
    top, bottom = pl.ds(0, 256), pl.ds(256, 256)
    c_h = [
        send(rsp.at[x2, :, q0], hap, to_x(1)),
        send(rsp.at[x2, :, q1], ham, to_x(3)),
        send(rsp.at[:, z2, q2], hbp, to_z(1)),
        send(rsp.at[:, z2, q3], hbm, to_z(3)),
    ]
    for c in c_sx:
        c.wait_recv()
    s1[...] = (sb[pl.ds(16 * core + 4 * x, 4)] + sx_r[0]) + (sx_r[1] + sx_r[2])
    c_sz = [send(s1.at[wrap(z + d)], sz_r.at[d - 1], to_z(d)) for d in (1, 3, 2)]
    t_on(5)
    t_own(6)

    def m_part(k):
        ms[k] = nn(ht[...], dys[k]) + ers[k].astype(F32)

    pl.loop(0, 2)(m_part)
    for c in c_h:
        c.wait_recv()
    rsp[x1, :, q0] = (rsf[x1, :, q0] + hap[...].astype(F32)).astype(BF)
    rsp[x3, :, q1] = (rsf[x3, :, q1] + ham[...].astype(F32)).astype(BF)
    rsp[:, z1, q2] = (rsf[:, z1, q2] + hbp[...].astype(F32)).astype(BF)
    rsp[:, z3, q3] = (rsf[:, z3, q3] + hbm[...].astype(F32)).astype(BF)
    c_r = {}

    def bulk(j):
        zj, xj = wrap(z + j), wrap(x + j)
        c_r[j] = [
            send(rsp.at[x1, zj, top], rap.at[j], to_x(1)),
            send(rsp.at[x3, zj, top], ram.at[j], to_x(3)),
            send(rsp.at[xj, z1, bottom], rbp.at[j], to_z(1)),
            send(rsp.at[xj, z3, bottom], rbm.at[j], to_z(3)),
        ]

    bulk(1)
    bulk(2)
    for c in c_sz:
        c.wait_recv()
    s2[...] = (s1[z] + sz_r[0]) + (sz_r[1] + sz_r[2])
    c_sy = [send(s2, sy_r.at[d - 1], to_y(d)) for d in (1, 3, 2)]
    t_on(6)
    t_own(7)
    for c in c_pgz:
        c.wait_recv()
    own = pl.ds(core * 48, 48)
    c_pgc = send(pg.at[own], pg.at[own], to_core)
    bulk(3)
    pl.loop(2, 4)(m_part)
    c_pgc.wait_recv()
    for i in range(12):
        ct[:, i] = jnp.transpose(pg[8 * i : 8 * i + 8], (1, 0, 2))
    lane = lax.broadcasted_iota(jnp.int32, (1, 128), 1)
    done_b, done_t = [], []

    def total(v):
        v = jnp.sum(v, axis=0)
        return jnp.sum(jnp.sum(v, axis=0, keepdims=True), axis=1, keepdims=True)

    for k in range(R):
        v = ct[k]
        t = jnp.where(lane == k, 1.0, 0.0)
        coeffs = [total(b * v) for b in done_b]
        for c, b, tb in zip(coeffs, done_b, done_t):
            v = v - c[None] * b
            t = t - c * tb
        scale = lax.rsqrt(total(v * v) + 1e-06)
        done_b.append(v * scale[None])
        done_t.append(t * scale)
        tt[k : k + 1, :] = done_t[-1]

    for c in c_sy:
        c.wait_recv()
    s = (s2[...] + sy_r[1]) + (sy_r[0] + sy_r[2])
    q = jnp.zeros((R, 128), F32)
    for i in range(R):
        q += tt[:, i : i + 1] * s[i : i + 1, :]
    mine = core * 16 + x * 4 + z
    sf[mine] = q * 0.25
    c_gz = [send(sf.at[mine], sf.at[mine], to_z(d)) for d in (1, 3, 2)]
    t_on(7)
    bulk(0)
    p = jnp.zeros((R, FP), F32)
    for i in range(R):
        p += tt[:, i : i + 1] * pf[i : i + 1, :]
    hi, mid, low = parts(p)
    rows = [hi, hi, mid, hi, low, mid] + [jnp.zeros_like(p)] * 10
    left[...] = jnp.concatenate(rows, axis=0).T.astype(BF)
    right[48:128, :] = jnp.zeros((80, D), BF)

    def right_part(b):
        hi, mid, low = parts(sf[b])
        r = jnp.concatenate([hi, mid, hi, low, hi, mid], axis=0).astype(BF)
        right[0:48, pl.ds(pl.multiple_of(b * 128, 128), 128)] = r

    for c in c_gz:
        c.wait_recv()
    own = pl.ds(core * 16 + x * 4, 4)
    c_gx = [send(sf.at[own], sf.at[own], to_x(d)) for d in (1, 3, 2)]

    c_za, c_xb = [], []
    for j in (1, 2, 3, 0):
        for c in c_r[j]:
            c.wait_recv()
        a = rsf[x, wrap(z + j), top] + (rap[j].astype(F32) + ram[j].astype(F32))
        b = rsf[wrap(x + j), z, bottom] + (rbp[j].astype(F32) + rbm[j].astype(F32))
        if j == 0:
            break
        a1[j] = a.astype(BF)
        b1[j] = b.astype(BF)
        c_za.append(send(a1.at[j], za_r.at[j - 1], to_z(j)))
        c_xb.append(send(b1.at[j], xb_r.at[j - 1], to_x(j)))
    for c in c_gx:
        c.wait_recv()
    own = pl.ds(core * 16, 16)
    c_gc = send(sf.at[own], sf.at[own], to_core)
    for i in range(16):
        right_part(core * 16 + i)
    for c in c_za:
        c.wait_recv()
    igs[0:256, :] = (
        (a + za_r[0].astype(F32)) + (za_r[1].astype(F32) + za_r[2].astype(F32))
    ).astype(BF)
    for c in c_xb:
        c.wait_recv()
    igs[256:512, :] = (
        (b + xb_r[0].astype(F32)) + (xb_r[1].astype(F32) + xb_r[2].astype(F32))
    ).astype(BF)
    c_gc.wait_recv()
    for i in range(16):
        right_part(other * 16 + i)
    for p in range(8):
        if p % 2 == 0:
            t_left[p].wait_recv()
        else:
            t_right[p].wait_recv()
    for c in t_far:
        c.wait_recv()
    for c in sent:
        c.wait_send()


def exchange(x, dy, wg, wu, wd, er, mo, q):
    v = pltpu.VMEM
    any_spec = pl.BlockSpec(memory_space=pl.ANY)
    vmem_spec = pl.BlockSpec(memory_space=pltpu.VMEM)
    scratch = [
        v((8, TOK, 512), BF), v((NK, TOK, KC), BF), v((16, 2, KP, 128), BF),
        v((NK, FP, KC), BF), v((NK, F, KC), BF), v((R, D), F32), v((16, KP, 128), BF),
        v((704, TOK), F32), v((FP, TOK), F32), v((F, TOK), BF), v((KP, TOK), F32),
        v((TOK, KP), BF), v((TOK, KP), BF), v((FP, 128), F32),
        v((R, FP), F32), v((3, R, FP), F32), v((32, FP), BF), v((R, FP), F32),
        v((96, 8, 128), F32), v((8, 12, 8, 128), F32), v((8, 128), F32),
        v((32, 8, 128), F32), v((16, 8, 128), F32), v((3, 4, 8, 128), F32),
        v((4, 8, 128), F32), v((3, 8, 128), F32), v((8, 128), F32), v((3, 8, 128), F32),
        v((32, 8, 128), F32),
        v((4, 4, TOK, 128), F32), v((4, 4, TOK, 128), BF),
        v((4, 128, 128), BF), v((4, 128, 128), BF), v((4, 128, 128), BF), v((4, 128, 128), BF),
        v((4, 256, 128), BF), v((4, 256, 128), BF), v((4, 256, 128), BF), v((4, 256, 128), BF),
        v((4, 256, 128), BF), v((4, 256, 128), BF), v((3, 256, 128), BF), v((3, 256, 128), BF),
        pltpu.SemaphoreType.DMA((88,)),
        pltpu.SemaphoreType.DMA((N_SEM,)),
        pltpu.SemaphoreType.DMA((N_SEM,)),
    ]
    out_shape = (
        v((TOK, 128), BF), v((4, 8, F, 128), BF), v((NK, F, KC), F32), v((F, KC), F32),
        v((FP, 128), BF), v((128, D), BF),
    )
    return pl.pallas_call(
        step_kernel,
        out_shape=out_shape,
        in_specs=[any_spec] * 8,
        out_specs=[vmem_spec] * 6,
        scratch_shapes=scratch,
        compiler_params=pltpu.CompilerParams(
            collective_id=0, has_side_effects=True, vmem_limit_bytes=48 * 1024 * 1024
        ),
        name="exchange",
    )(x, dy, wg, wu, wd, er, mo, q)


def apply_kernel(ig, t_ref, m_ref, mo_ref, left, right, ig_o, nd_o, ne_o, nm_o, nd, ne, nm, sem):
    dp = lax.axis_index("dp")
    out_ig = pltpu.make_async_copy(ig, ig_o, sem.at[0])
    out_ig.start()
    l = left[0:F, :]
    copies = [out_ig]
    for j in range(8):
        cols = slice(j * 512, (j + 1) * 512)
        approx = nn(l, right[:, cols])
        half = slice((j % 2) * 512, (j % 2) * 512 + 512)
        ne[:, cols] = (m_ref[j // 2, :, half] - approx).astype(BF)
        for c in range(4):
            lanes = slice(c * 128, (c + 1) * 128)
            b = 4 * j + c
            nd[:, b * 128 : (b + 1) * 128] = (
                t_ref[b // 8, b % 8].astype(F32) - 0.1 * approx[:, lanes]
            ).astype(BF)
        for n, (src, dst) in enumerate(((ne, ne_o), (nd, nd_o))):
            copies.append(
                pltpu.make_async_copy(
                    src.at[:, pl.ds(j * 512, 512)], dst.at[:, pl.ds(j * 512, 512)],
                    sem.at[1 + 2 * j + n],
                )
            )
            copies[-1].start()
        if j % 4 == 1:
            h = j // 4
            cols = pl.ds(pl.multiple_of(dp * KC + h * 512, 512), 512)
            nm[:, h * 512 : (h + 1) * 512] = 0.9 * mo_ref[:, h * 512 : (h + 1) * 512] + nn(
                l, right[:, cols]
            )
            copies.append(
                pltpu.make_async_copy(
                    nm.at[:, pl.ds(h * 512, 512)], nm_o.at[:, pl.ds(h * 512, 512)], sem.at[17 + h]
                )
            )
            copies[-1].start()
    for c in copies:
        c.wait()


def apply(*args):
    v = pltpu.VMEM
    args = [pltpu.with_memory_space_constraint(a, pltpu.VMEM) for a in args]
    return pl.pallas_call(
        apply_kernel,
        out_shape=(
            jax.ShapeDtypeStruct((TOK, 128), BF),
            jax.ShapeDtypeStruct((F, D), BF),
            jax.ShapeDtypeStruct((F, D), BF),
            jax.ShapeDtypeStruct((F, KC), F32),
        ),
        in_specs=[pl.BlockSpec(memory_space=pltpu.VMEM)] * len(args),
        out_specs=[pl.BlockSpec(memory_space=pl.ANY)] * 4,
        scratch_shapes=[
            v((F, D), BF), v((F, D), BF), v((F, KC), F32), pltpu.SemaphoreType.DMA((20,)),
        ],
        compiler_params=pltpu.CompilerParams(vmem_limit_bytes=24 * 1024 * 1024),
        name="apply",
    )(*args)


def body(inputs, out_grads, w_gate, w_up, w_down, err_down, mom_down, q_down):
    kept = exchange(
        inputs, out_grads, w_gate.T, w_up.T, w_down, err_down[0], mom_down, q_down.T
    )
    ig, nd, ne, nm = apply(*kept)
    return ig, nd, ne[None], nm


def solution(mesh):
    in_specs = (
        P("dp", None), P("dp", None), P(None, "mp"), P(None, "mp"), P("mp", None),
        P("dp", "mp", None), P("mp", "dp"), P(),
    )
    out_specs = (P("dp", "mp"), P("mp", None), P("dp", "mp", None), P("mp", "dp"))
    return jax.shard_map(body, mesh=mesh, in_specs=in_specs, out_specs=out_specs, check_vma=False)
```

time: 70.9 us -> 54.7 us (0.77)
  Pallas kernels: 69.8 us -> 53.4 us
    pallas_call x1, Pallas kernels: 59.5 us -> 50.1 us  [exchange(): pl.pallas_call(step_kernel, out_shape=out_shape, in_specs=[any_spec] * 8,...]
    pallas_call x1, Pallas kernels: 10.2 us -> 3.32 us  [apply(): pl.pallas_call(apply_kernel, out_shape=(jax.ShapeDtypeStruct((TOK, 128),...]
where the time goes in v2:
time: 54.7 us; the launch traced here: 54.1 us
  Pallas kernels  53.4 us (98%)
  between operations  0.64 us (1%)
    pallas_call x1, Pallas kernels, exchange(): pl.pallas_call(step_kernel, out_shape=out_shape, in_specs=[any_spec] * 8,...  50.1 us
    pallas_call x1, Pallas kernels, apply(): pl.pallas_call(apply_kernel, out_shape=(jax.ShapeDtypeStruct((TOK, 128),...  3.32 us

profile of v2, /device:TPU:0, one launch (start us, length us, event | category | flops | bytes accessed | tf_op | source)
XLA Modules:
  0.0 54.1 jit_solution(12444959683364389473)
XLA Ops:
  0.6 50.1 %exchange.1 = (bf16[512,128]{1,0:T(8,128)(2,1)S(1)}, bf16[4,8,344,128]{3,2,1,0:T(8,128)(2,1)S(1)}, f32[4,344,1024]{2,1,0:T(8,128)S(1)}, f32[344,1024]{1,0:T(8,12...) custom-call(bf16[512,4096]{1,0:T(8,128)(2,1)} %x_h.1, bf16[512,4096]{1,0:T(8,128)(2,1)} %dy_h.1, ...), custom_call_target="tpu_custom_call" | custom-call | tf_op jit(solution)/shard_map/exchange/pallas_call | solution.py:450
  50.7 3.3 %apply.1 = (bf16[512,128]{1,0:T(8,128)(2,1)}, bf16[344,4096]{1,0:T(8,128)(2,1)}, bf16[344,4096]{1,0:T(8,128)(2,1)}, f32[344,1024]{1,0:T(8,128)}) custom-call(bf16[512,128]{1,0:T(8,128)(2,1)S(1)} %get-tuple-element.14.ig, bf16[4,8,344,128]{3,2,1,0:T(8,128)(2,1)S(1)} %get-tuple-element.15.t_ref, f32[4,344,1024]{2,1,0:T(8,128)S(1)} %get-tuple-element.16.m_ref, ...), custom_call_target="tpu_custom_call" | custom-call | tf_op jit(solution)/shard_map/apply/pallas_call | solution.py:507

commit v3 on v2

v3 whole, which is shorter than its diff:
```python
import jax
import jax.numpy as jnp
from jax import lax
from jax.experimental import pallas as pl
from jax.experimental.pallas import tpu as pltpu
from jax.sharding import PartitionSpec as P

MESH = pl.DeviceIdType.MESH
BF = jnp.bfloat16
F32 = jnp.float32
TOK, D, F, FP, R = 512, 4096, 344, 384, 8
UP = 352
KP = 768
KC = 1024
NK = D // KC
N_SEM = 32
PLANE = [(i, j) for i in range(4) for j in range(4) if i or j]


def nt(a, b):
    return lax.dot_general(a, b, (((1,), (1,)), ((), ())), preferred_element_type=F32)


def nn(a, b):
    return lax.dot_general(a, b, (((1,), (0,)), ((), ())), preferred_element_type=F32)


def parts(v):
    hi = v.astype(BF).astype(F32)
    rest = v - hi
    mid = rest.astype(BF).astype(F32)
    return hi, mid, rest - mid


def split3(v):
    hi, mid, low = parts(v)
    return jnp.concatenate([hi, mid, low, jnp.zeros_like(v)], axis=0).astype(BF)


def fold(r):
    return (r[0:8] + r[8:16]) + r[16:24]


def wrap(v):
    return lax.rem(v, 4)


def step_kernel(
    x_h, dy_h, wg_h, wu_h, wd_h, er_h, mo_h, q_h,
    igs, tg, ms, mos, left, right,
    xs, dys, ws, wds, ers, qs, wsp,
    gu, dhq, ht, dt, dc, dcp, erq,
    pown, py_r, p3, pf, pg, ct, tt,
    sb, sc_r, sp_r, s2, sy_r, sf,
    rsf, rsp, rr, a1, b1, zx,
    load_sem, send_sem, recv_sem,
):
    dp = lax.axis_index("dp")
    mp = lax.axis_index("mp")
    core = lax.rem(mp, 2)
    z = lax.rem(mp // 2, 4)
    x = mp // 8
    other = 1 - core
    to_core = (dp, mp + 1 - 2 * core)

    def to_x(d):
        return (dp, wrap(x + d) * 8 + z * 2 + core)

    def to_z(d):
        return (dp, x * 8 + wrap(z + d) * 2 + core)

    def to_y(d):
        return (wrap(dp + d), mp)

    def to_plane(i, j):
        return (dp, wrap(x + i) * 8 + wrap(z + j) * 2 + core)

    barrier = pltpu.get_barrier_semaphore()
    peers = [to_core] + [to_plane(i, j) for i, j in PLANE] + [to_y(d) for d in (1, 2, 3)]
    for peer in peers:
        pl.semaphore_signal(barrier, inc=1, device_id=peer, device_id_type=MESH)

    def lx(k):
        cols = pl.ds(k * 512, 512)
        return pltpu.make_async_copy(x_h.at[:, cols], xs.at[k], load_sem.at[k])

    def lwg(k):
        cols = pl.ds(k * 512, 512)
        return pltpu.make_async_copy(wg_h.at[:, cols], ws.at[k, pl.ds(0, F)], load_sem.at[8 + k])

    def lwu(k):
        cols = pl.ds(k * 512, 512)
        return pltpu.make_async_copy(wu_h.at[:, cols], ws.at[k, pl.ds(UP, F)], load_sem.at[16 + k])

    def ly(k):
        return pltpu.make_async_copy(dy_h.at[:, pl.ds(k * KC, KC)], dys.at[k], load_sem.at[24 + k])

    def lwd(k):
        return pltpu.make_async_copy(
            wd_h.at[:, pl.ds(k * KC, KC)], wds.at[k, pl.ds(0, F)], load_sem.at[28 + k]
        )

    def ler(k):
        return pltpu.make_async_copy(er_h.at[:, pl.ds(k * KC, KC)], ers.at[k], load_sem.at[32])

    lmo = pltpu.make_async_copy(mo_h, mos, load_sem.at[33])
    lq = pltpu.make_async_copy(q_h, qs, load_sem.at[34])
    for k in range(8):
        lx(k).start()
        lwg(k).start()
        lwu(k).start()
        if k == 1:
            lmo.start()
            lwd(dp).start()
    lq.start()
    ly(dp).start()
    for i in range(1, NK):
        ly(wrap(dp + i)).start()
        lwd(wrap(dp + i)).start()
    for k in range(NK):
        ler(k).start()

    count = [0]
    sent = []

    class Exchange:
        def __init__(self, whole):
            i = count[0]
            count[0] += 1
            self.sems = send_sem.at[i], recv_sem.at[i]
            self.whole = whole
            sent.append(self)

        def send(self, src, dst, device):
            pltpu.make_async_remote_copy(
                src_ref=src, dst_ref=dst, send_sem=self.sems[0], recv_sem=self.sems[1],
                device_id=device, device_id_type=MESH,
            ).start()
            return self

        def wait_send(self):
            pltpu.make_async_copy(self.whole, self.whole, self.sems[0]).wait()

        def wait_recv(self):
            pltpu.make_async_copy(self.whole, self.whole, self.sems[1]).wait()

    def send(src, dst, device):
        return Exchange(dst).send(src, dst, device)

    for ref in (gu, dhq, erq, pown):
        ref[...] = jnp.zeros_like(ref)
    ws[:, F:UP, :] = jnp.zeros((8, UP - F, 512), BF)
    ws[:, UP + F :, :] = jnp.zeros((8, KP - UP - F, 512), BF)
    wds[:, F:UP, :] = jnp.zeros((NK, UP - F, KC), BF)
    dt[F:UP, :] = jnp.zeros((UP - F, TOK), dt.dtype)
    dt[UP + F :, :] = jnp.zeros((KP - UP - F, TOK), dt.dtype)

    def arrived(k):
        lx(k).wait()
        lwg(k).wait()
        lwu(k).wait()

    @pl.loop(0, 2)
    def _(k):
        arrived(k)
        gu[...] += nt(ws[k, 0:704], xs[k])

    pl.semaphore_wait(barrier, len(peers))
    lmo.wait()
    lwd(dp).wait()
    for p in range(8):
        lanes = pl.ds(p * 128, 128)
        tg[dp, p] = (wds[dp, 0:F, lanes].astype(F32) - 0.1 * (0.9 * mos[:, lanes])).astype(BF)
    y_right, y_left = wrap(dp + 1), wrap(dp + 3)

    def t_own(lo, n):
        at = tg.at[dp, pl.ds(lo, n)]
        return send(at, at, to_y(1)), send(at, at, to_y(3))

    def t_right(lo, n):
        at = tg.at[y_left, pl.ds(lo, n)]
        return send(at, at, to_y(1))

    def t_left(lo, n):
        at = tg.at[y_right, pl.ds(lo, n)]
        return send(at, at, to_y(3))

    t0 = t_own(0, 4)

    @pl.loop(1, 4)
    def _(k):
        arrived(2 * k)
        arrived(2 * k + 1)
        w = jnp.concatenate([ws[2 * k, 0:704], ws[2 * k + 1, 0:704]], axis=1)
        gu[...] += nt(w, jnp.concatenate([xs[2 * k], xs[2 * k + 1]], axis=1))

    def half_lanes(c, n):
        return pl.ds(pl.multiple_of(c * 128 + n * 256, 128), 128)

    c_w = Exchange(wsp)
    for n in range(2):
        c_w.send(ws.at[:, :, half_lanes(other, n)], wsp.at[:, :, pl.ds(n * 128, 128)], to_core)

    lq.wait()
    for k in range(NK):
        wds[k, UP:FP, :] = split3(qs[:, k * KC : (k + 1) * KC])

    @pl.loop(0, NK)
    def _(i):
        k = wrap(dp + i)
        ly(k).wait()

        @pl.when(i > 0)
        def _():
            lwd(k).wait()

        dhq[...] += nt(wds[k], dys[k])

    pltpu.make_async_copy(er_h, er_h, load_sem.at[32]).wait()

    @pl.loop(0, NK)
    def _(k):
        erq[0:F, 0:32] += nt(ers[k], wds[k, UP:FP, :])

    @pl.loop(0, 4)
    def _(i):
        lanes = pl.ds(pl.multiple_of(i * 128, 128), 128)
        gv, uv, dv = gu[0:F, lanes], gu[UP : UP + F, lanes], dhq[0:F, lanes]
        sig = jax.nn.sigmoid(gv)
        gs = gv * sig
        ht[:, lanes] = (gs * uv).astype(BF)
        dt[0:F, lanes] = (dv * uv * sig * (1.0 + gv * (1.0 - sig))).astype(dt.dtype)
        dt[UP : UP + F, lanes] = (dv * gs).astype(dt.dtype)

    own_p = fold(nt(split3(fold(dhq[UP:FP, :])), ht[...]))
    pown[:, 0:F] = own_p + fold(erq[...].T[0:32, 0:F])
    c_py = Exchange(py_r)
    for d in (1, 3, 2):
        c_py.send(pown, py_r.at[d - 1], to_y(d))
    t1 = t_own(4, 2)

    dc[...] = dt[...].T.astype(BF)
    c_dc = send(dc, dcp, to_core)

    @pl.loop(0, 4)
    def _(i):
        w = [ws[2 * i + n // 2, :, half_lanes(core, n % 2)] for n in range(4)]
        r = nn(dc[...], jnp.concatenate(w, axis=1))
        for n in range(4):
            rsf[i, n] = r[:, n * 128 : (n + 1) * 128]

    t0[0].wait_recv()
    t0[1].wait_recv()
    far = [t_right(0, 2), t_left(2, 2)]
    t2 = t_own(6, 1)
    c_py.wait_recv()
    pf[...] = ((pown[...] + py_r[1]) + (py_r[0] + py_r[2])) * 0.25
    base = core * 48 + z * 12
    for c in range(3):
        pg[base + x * 3 + c] = pf[:, c * 128 : (c + 1) * 128]
    own = pl.ds(base + x * 3, 3)
    c_pg = Exchange(pg.at[pl.ds(0, 45)])
    for i, j in PLANE:
        c_pg.send(pg.at[own], pg.at[own], to_plane(i, j))
    p3[...] = split3(pf[...])
    hp3 = split3(fold(nn(p3[:, 0:F], ht[...])))

    def s_part(c):
        s = fold(nn(hp3, dys[c]) + nn(p3[:, 0:F], ers[c]))
        for j in range(8):
            sb[8 * c + j] = s[:, j * 128 : (j + 1) * 128]

    s_part(2 * other)
    s_part(2 * other + 1)
    c_sc = send(sb.at[pl.ds(16 * other, 16)], sc_r, to_core)
    s_part(2 * core)
    s_part(2 * core + 1)

    c_w.wait_recv()
    c_dc.wait_recv()

    def rs_peer(i):
        r = nn(dcp[...], jnp.concatenate([wsp[2 * i], wsp[2 * i + 1]], axis=1))
        for n in range(4):
            v = rsf[i, n] + r[:, n * 128 : (n + 1) * 128]
            rsf[i, n] = v
            rsp[i, n] = v.astype(BF)

    pl.loop(0, 2)(rs_peer)
    c_sc.wait_recv()
    half = pl.ds(16 * core, 16)
    sb[half] = sb[half] + sc_r[...]
    c_sp = Exchange(sp_r)
    for i, j in PLANE:
        c_sp.send(
            sb.at[16 * core + 4 * wrap(x + i) + wrap(z + j)], sp_r.at[4 * i + j - 1], to_plane(i, j)
        )
    pl.loop(2, 4)(rs_peer)
    top, bottom = pl.ds(0, 256), pl.ds(256, 256)
    c_r = {}

    def bulk(j):
        zj, xj = wrap(z + j), wrap(x + j)
        c_r[j] = Exchange(rr.at[j])
        for d in (1, 3, 2):
            c_r[j].send(rsp.at[wrap(x + d), zj, top], rr.at[j, d - 1], to_x(d))
            c_r[j].send(rsp.at[xj, wrap(z + d), bottom], rr.at[j, d + 2], to_z(d))

    bulk(1)
    bulk(2)
    c_pg.wait_recv()
    own = pl.ds(core * 48, 48)
    c_pgc = send(pg.at[own], pg.at[own], to_core)
    c_sp.wait_recv()
    mine = core * 16 + x * 4 + z
    s2[...] = jnp.sum(sp_r[...], axis=0) + sb[mine]
    c_sy = Exchange(sy_r)
    for d in (1, 3, 2):
        c_sy.send(s2, sy_r.at[d - 1], to_y(d))
    t3 = t_own(7, 1)
    t1[0].wait_recv()
    far.append(t_right(4, 1))
    t1[1].wait_recv()
    far.append(t_left(5, 1))

    c_pgc.wait_recv()
    for i in range(12):
        ct[:, i] = jnp.transpose(pg[8 * i : 8 * i + 8], (1, 0, 2))
    lane = lax.broadcasted_iota(jnp.int32, (1, 128), 1)
    done_b, done_t = [], []

    def total(v):
        v = jnp.sum(v, axis=0)
        return jnp.sum(jnp.sum(v, axis=0, keepdims=True), axis=1, keepdims=True)

    for k in range(R):
        v = ct[k]
        t = jnp.where(lane == k, 1.0, 0.0)
        coeffs = [total(b * v) for b in done_b]
        for c, b, tb in zip(coeffs, done_b, done_t):
            v = v - c[None] * b
            t = t - c * tb
        scale = lax.rsqrt(total(v * v) + 1e-06)
        done_b.append(v * scale[None])
        done_t.append(t * scale)
        tt[k : k + 1, :] = done_t[-1]

    c_sy.wait_recv()
    s = (s2[...] + sy_r[1]) + (sy_r[0] + sy_r[2])
    q = jnp.zeros((R, 128), F32)
    for i in range(R):
        q += tt[:, i : i + 1] * s[i : i + 1, :]
    sf[mine] = q * 0.25
    c_g = Exchange(sf.at[pl.ds(0, 15)])
    for i, j in PLANE:
        c_g.send(sf.at[mine], sf.at[mine], to_plane(i, j))
    bulk(3)
    bulk(0)
    t2[0].wait_recv()
    far.append(t_right(6, 1))

    @pl.loop(0, NK)
    def _(k):
        ms[k] = nn(ht[...], dys[k]) + ers[k].astype(F32)

    c_zx = Exchange(zx)

    def first_sums(j):
        c_r[j].wait_recv()
        a = rsf[x, wrap(z + j), top]
        b = rsf[wrap(x + j), z, bottom]
        for d in range(3):
            a += rr[j, d].astype(F32)
            b += rr[j, d + 3].astype(F32)
        return a, b

    def second(j):
        a, b = first_sums(j)
        a1[j] = a.astype(BF)
        b1[j] = b.astype(BF)
        c_zx.send(a1.at[j], zx.at[j - 1], to_z(j))
        c_zx.send(b1.at[j], zx.at[j + 2], to_x(j))

    second(1)
    second(2)
    t3[1].wait_recv()
    far.append(t_left(7, 1))

    p = jnp.zeros((R, FP), F32)
    for i in range(R):
        p += tt[:, i : i + 1] * pf[i : i + 1, :]
    hi, mid, low = parts(p)
    rows = [hi, hi, mid, hi, low, mid] + [jnp.zeros_like(p)] * 10
    left[...] = jnp.concatenate(rows, axis=0).T.astype(BF)
    right[48:128, :] = jnp.zeros((80, D), BF)

    def right_part(b):
        hi, mid, low = parts(sf[b])
        r = jnp.concatenate([hi, mid, hi, low, hi, mid], axis=0).astype(BF)
        right[0:48, pl.ds(pl.multiple_of(b * 128, 128), 128)] = r

    c_g.wait_recv()
    own = pl.ds(core * 16, 16)
    c_gc = send(sf.at[own], sf.at[own], to_core)
    for i in range(16):
        right_part(core * 16 + i)
    second(3)
    a, b = first_sums(0)
    c_gc.wait_recv()
    for i in range(16):
        right_part(other * 16 + i)
    c_zx.wait_recv()
    for d in range(3):
        a += zx[d].astype(F32)
        b += zx[d + 3].astype(F32)
    igs[0:256, :] = a.astype(BF)
    igs[256:512, :] = b.astype(BF)
    for c in (t2[1], t3[0], *far):
        c.wait_recv()
    for c in sent:
        c.wait_send()


def exchange(x, dy, wg, wu, wd, er, mo, q):
    v = pltpu.VMEM
    any_spec = pl.BlockSpec(memory_space=pl.ANY)
    vmem_spec = pl.BlockSpec(memory_space=pltpu.VMEM)
    scratch = [
        v((8, TOK, 512), BF), v((NK, TOK, KC), BF), v((8, KP, 512), BF),
        v((NK, FP, KC), BF), v((NK, F, KC), BF), v((R, D), F32), v((8, KP, 256), BF),
        v((704, TOK), F32), v((FP, TOK), F32), v((F, TOK), BF), v((KP, TOK), F32),
        v((TOK, KP), BF), v((TOK, KP), BF), v((FP, 128), F32),
        v((R, FP), F32), v((3, R, FP), F32), v((32, FP), BF), v((R, FP), F32),
        v((96, 8, 128), F32), v((8, 12, 8, 128), F32), v((8, 128), F32),
        v((32, 8, 128), F32), v((16, 8, 128), F32), v((15, 8, 128), F32),
        v((8, 128), F32), v((3, 8, 128), F32), v((32, 8, 128), F32),
        v((4, 4, TOK, 128), F32), v((4, 4, TOK, 128), BF), v((4, 6, 256, 128), BF),
        v((4, 256, 128), BF), v((4, 256, 128), BF), v((6, 256, 128), BF),
        pltpu.SemaphoreType.DMA((35,)),
        pltpu.SemaphoreType.DMA((N_SEM,)),
        pltpu.SemaphoreType.DMA((N_SEM,)),
    ]
    out_shape = (
        v((TOK, 128), BF), v((4, 8, F, 128), BF), v((NK, F, KC), F32), v((F, KC), F32),
        v((FP, 128), BF), v((128, D), BF),
    )
    return pl.pallas_call(
        step_kernel,
        out_shape=out_shape,
        in_specs=[any_spec] * 8,
        out_specs=[vmem_spec] * 6,
        scratch_shapes=scratch,
        compiler_params=pltpu.CompilerParams(
            collective_id=0, has_side_effects=True, vmem_limit_bytes=48 * 1024 * 1024
        ),
        name="exchange",
    )(x, dy, wg, wu, wd, er, mo, q)


def apply_kernel(ig, t_ref, m_ref, mo_ref, left, right, ig_o, nd_o, ne_o, nm_o, nd, ne, nm, sem):
    dp = lax.axis_index("dp")
    out_ig = pltpu.make_async_copy(ig, ig_o, sem.at[0])
    out_ig.start()
    l = left[0:F, :]
    copies = [out_ig]
    for j in range(8):
        cols = slice(j * 512, (j + 1) * 512)
        approx = nn(l, right[:, cols])
        half = slice((j % 2) * 512, (j % 2) * 512 + 512)
        ne[:, cols] = (m_ref[j // 2, :, half] - approx).astype(BF)
        for c in range(4):
            lanes = slice(c * 128, (c + 1) * 128)
            b = 4 * j + c
            nd[:, b * 128 : (b + 1) * 128] = (
                t_ref[b // 8, b % 8].astype(F32) - 0.1 * approx[:, lanes]
            ).astype(BF)
        for n, (src, dst) in enumerate(((ne, ne_o), (nd, nd_o))):
            copies.append(
                pltpu.make_async_copy(
                    src.at[:, pl.ds(j * 512, 512)], dst.at[:, pl.ds(j * 512, 512)],
                    sem.at[1 + 2 * j + n],
                )
            )
            copies[-1].start()
        if j % 4 == 1:
            h = j // 4
            cols = pl.ds(pl.multiple_of(dp * KC + h * 512, 512), 512)
            nm[:, h * 512 : (h + 1) * 512] = 0.9 * mo_ref[:, h * 512 : (h + 1) * 512] + nn(
                l, right[:, cols]
            )
            copies.append(
                pltpu.make_async_copy(
                    nm.at[:, pl.ds(h * 512, 512)], nm_o.at[:, pl.ds(h * 512, 512)], sem.at[17 + h]
                )
            )
            copies[-1].start()
    for c in copies:
        c.wait()


def apply(*args):
    v = pltpu.VMEM
    args = [pltpu.with_memory_space_constraint(a, pltpu.VMEM) for a in args]
    return pl.pallas_call(
        apply_kernel,
        out_shape=(
            jax.ShapeDtypeStruct((TOK, 128), BF),
            jax.ShapeDtypeStruct((F, D), BF),
            jax.ShapeDtypeStruct((F, D), BF),
            jax.ShapeDtypeStruct((F, KC), F32),
        ),
        in_specs=[pl.BlockSpec(memory_space=pltpu.VMEM)] * len(args),
        out_specs=[pl.BlockSpec(memory_space=pl.ANY)] * 4,
        scratch_shapes=[
            v((F, D), BF), v((F, D), BF), v((F, KC), F32), pltpu.SemaphoreType.DMA((20,)),
        ],
        compiler_params=pltpu.CompilerParams(vmem_limit_bytes=24 * 1024 * 1024),
        name="apply",
    )(*args)


def body(inputs, out_grads, w_gate, w_up, w_down, err_down, mom_down, q_down):
    kept = exchange(
        inputs, out_grads, w_gate.T, w_up.T, w_down, err_down[0], mom_down, q_down.T
    )
    ig, nd, ne, nm = apply(*kept)
    return ig, nd, ne[None], nm


def solution(mesh):
    in_specs = (
        P("dp", None), P("dp", None), P(None, "mp"), P(None, "mp"), P("mp", None),
        P("dp", "mp", None), P("mp", "dp"), P(),
    )
    out_specs = (P("dp", "mp"), P("mp", None), P("dp", "mp", None), P("mp", "dp"))
    return jax.shard_map(body, mesh=mesh, in_specs=in_specs, out_specs=out_specs, check_vma=False)
```

time: 54.7 us -> 45.8 us (0.84)
  Pallas kernels: 53.4 us -> 45 us
    pallas_call x1, Pallas kernels: 50.1 us -> 41.7 us  [exchange(): pl.pallas_call(step_kernel, out_shape=out_shape, in_specs=[any_spec] * 8,...]
where the time goes in v3:
time: 45.8 us; the launch traced here: 45.7 us
  Pallas kernels  45 us (98%)
  between operations  0.64 us (1%)
    pallas_call x1, Pallas kernels, exchange(): pl.pallas_call(step_kernel, out_shape=out_shape, in_specs=[any_spec] * 8,...  41.7 us
    pallas_call x1, Pallas kernels, apply(): pl.pallas_call(apply_kernel, out_shape=(jax.ShapeDtypeStruct((TOK, 128),...  3.32 us

profile of v3, /device:TPU:0, one launch (start us, length us, event | category | flops | bytes accessed | tf_op | source)
XLA Modules:
  0.0 45.7 jit_solution(9396768091947507354)
XLA Ops:
  0.6 41.7 %exchange.1 = (bf16[512,128]{1,0:T(8,128)(2,1)S(1)}, bf16[4,8,344,128]{3,2,1,0:T(8,128)(2,1)S(1)}, f32[4,344,1024]{2,1,0:T(8,128)S(1)}, f32[344,1024]{1,0:T(8,12...) custom-call(bf16[512,4096]{1,0:T(8,128)(2,1)} %x_h.1, bf16[512,4096]{1,0:T(8,128)(2,1)} %dy_h.1, ...), custom_call_target="tpu_custom_call" | custom-call | tf_op jit(solution)/shard_map/exchange/pallas_call | solution.py:447
  42.4 3.3 %apply.1 = (bf16[512,128]{1,0:T(8,128)(2,1)}, bf16[344,4096]{1,0:T(8,128)(2,1)}, bf16[344,4096]{1,0:T(8,128)(2,1)}, f32[344,1024]{1,0:T(8,128)}) custom-call(bf16[512,128]{1,0:T(8,128)(2,1)S(1)} %get-tuple-element.14.ig, bf16[4,8,344,128]{3,2,1,0:T(8,128)(2,1)S(1)} %get-tuple-element.15.t_ref, f32[4,344,1024]{2,1,0:T(8,128)S(1)} %get-tuple-element.16.m_ref, ...), custom_call_target="tpu_custom_call" | custom-call | tf_op jit(solution)/shard_map/apply/pallas_call | solution.py:504

commit v4 on v3

--- a/solution.py
+++ b/solution.py
@@ -13,7 +13,7 @@
 KP = 768
 KC = 1024
 NK = D // KC
-N_SEM = 32
+N_SEM = 34
 PLANE = [(i, j) for i in range(4) for j in range(4) if i or j]
 
 
@@ -47,12 +47,12 @@
 
 def step_kernel(
     x_h, dy_h, wg_h, wu_h, wd_h, er_h, mo_h, q_h,
-    igs, tg, ms, mos, left, right,
+    igs, ne, tg, ms, mos, left, right,
     xs, dys, ws, wds, ers, qs, wsp,
     gu, dhq, ht, dt, dc, dcp, erq,
     pown, py_r, p3, pf, pg, ct, tt,
     sb, sc_r, sp_r, s2, sy_r, sf,
-    rsf, rsp, rr, a1, b1, zx,
+    rsf, rsp, ha, hb, ra, rb, a1, b1, zx,
     load_sem, send_sem, recv_sem,
 ):
     dp = lax.axis_index("dp")
@@ -80,36 +80,45 @@
     for peer in peers:
         pl.semaphore_signal(barrier, inc=1, device_id=peer, device_id_type=MESH)
 
+    def group(k):
+        return k if k < 2 else 1 + k // 2
+
     def lx(k):
         cols = pl.ds(k * 512, 512)
-        return pltpu.make_async_copy(x_h.at[:, cols], xs.at[k], load_sem.at[k])
+        return pltpu.make_async_copy(x_h.at[:, cols], xs.at[k], load_sem.at[group(k)])
 
     def lwg(k):
         cols = pl.ds(k * 512, 512)
-        return pltpu.make_async_copy(wg_h.at[:, cols], ws.at[k, pl.ds(0, F)], load_sem.at[8 + k])
+        return pltpu.make_async_copy(wg_h.at[:, cols], ws.at[k, pl.ds(0, F)], load_sem.at[5 + group(k)])
 
     def lwu(k):
         cols = pl.ds(k * 512, 512)
-        return pltpu.make_async_copy(wu_h.at[:, cols], ws.at[k, pl.ds(UP, F)], load_sem.at[16 + k])
+        return pltpu.make_async_copy(wu_h.at[:, cols], ws.at[k, pl.ds(UP, F)], load_sem.at[5 + group(k)])
+
+    def arrived(k, n, sem):
+        at = xs.at[pl.ds(k, n)]
+        pltpu.make_async_copy(at, at, load_sem.at[sem]).wait()
+        at = ws.at[pl.ds(k, n), pl.ds(0, 2 * F)]
+        pltpu.make_async_copy(at, at, load_sem.at[5 + sem]).wait()
 
     def ly(k):
-        return pltpu.make_async_copy(dy_h.at[:, pl.ds(k * KC, KC)], dys.at[k], load_sem.at[24 + k])
+        return pltpu.make_async_copy(dy_h.at[:, pl.ds(k * KC, KC)], dys.at[k], load_sem.at[10 + k])
 
     def lwd(k):
         return pltpu.make_async_copy(
-            wd_h.at[:, pl.ds(k * KC, KC)], wds.at[k, pl.ds(0, F)], load_sem.at[28 + k]
+            wd_h.at[:, pl.ds(k * KC, KC)], wds.at[k, pl.ds(0, F)], load_sem.at[14 + k]
         )
 
     def ler(k):
-        return pltpu.make_async_copy(er_h.at[:, pl.ds(k * KC, KC)], ers.at[k], load_sem.at[32])
-
-    lmo = pltpu.make_async_copy(mo_h, mos, load_sem.at[33])
-    lq = pltpu.make_async_copy(q_h, qs, load_sem.at[34])
+        return pltpu.make_async_copy(er_h.at[:, pl.ds(k * KC, KC)], ers.at[k], load_sem.at[18])
+
+    lmo = pltpu.make_async_copy(mo_h, mos, load_sem.at[19])
+    lq = pltpu.make_async_copy(q_h, qs, load_sem.at[20])
     for k in range(8):
         lx(k).start()
         lwg(k).start()
         lwu(k).start()
-        if k == 1:
+        if k == 3:
             lmo.start()
             lwd(dp).start()
     lq.start()
@@ -155,16 +164,17 @@
     dt[F:UP, :] = jnp.zeros((UP - F, TOK), dt.dtype)
     dt[UP + F :, :] = jnp.zeros((KP - UP - F, TOK), dt.dtype)
 
-    def arrived(k):
-        lx(k).wait()
-        lwg(k).wait()
-        lwu(k).wait()
-
     @pl.loop(0, 2)
     def _(k):
-        arrived(k)
+        arrived(k, 1, k)
         gu[...] += nt(ws[k, 0:704], xs[k])
 
+    def gate_up(k):
+        arrived(2 * k, 2, 1 + k)
+        w = jnp.concatenate([ws[2 * k, 0:704], ws[2 * k + 1, 0:704]], axis=1)
+        gu[...] += nt(w, jnp.concatenate([xs[2 * k], xs[2 * k + 1]], axis=1))
+
+    pl.loop(1, 2)(gate_up)
     pl.semaphore_wait(barrier, len(peers))
     lmo.wait()
     lwd(dp).wait()
@@ -185,14 +195,9 @@
         at = tg.at[y_right, pl.ds(lo, n)]
         return send(at, at, to_y(3))
 
-    t0 = t_own(0, 4)
-
-    @pl.loop(1, 4)
-    def _(k):
-        arrived(2 * k)
-        arrived(2 * k + 1)
-        w = jnp.concatenate([ws[2 * k, 0:704], ws[2 * k + 1, 0:704]], axis=1)
-        gu[...] += nt(w, jnp.concatenate([xs[2 * k], xs[2 * k + 1]], axis=1))
+    t0 = t_own(0, 3)
+
+    pl.loop(2, 4)(gate_up)
 
     def half_lanes(c, n):
         return pl.ds(pl.multiple_of(c * 128 + n * 256, 128), 128)
@@ -205,22 +210,26 @@
     for k in range(NK):
         wds[k, UP:FP, :] = split3(qs[:, k * KC : (k + 1) * KC])
 
-    @pl.loop(0, NK)
+    @pl.loop(0, 2)
     def _(i):
-        k = wrap(dp + i)
+        k, n = wrap(dp + 2 * i), wrap(dp + 2 * i + 1)
         ly(k).wait()
+        ly(n).wait()
+        lwd(n).wait()
 
         @pl.when(i > 0)
         def _():
             lwd(k).wait()
 
-        dhq[...] += nt(wds[k], dys[k])
-
-    pltpu.make_async_copy(er_h, er_h, load_sem.at[32]).wait()
-
-    @pl.loop(0, NK)
-    def _(k):
-        erq[0:F, 0:32] += nt(ers[k], wds[k, UP:FP, :])
+        dhq[...] += nt(
+            jnp.concatenate([wds[k], wds[n]], axis=1), jnp.concatenate([dys[k], dys[n]], axis=1)
+        )
+
+    pltpu.make_async_copy(er_h, er_h, load_sem.at[18]).wait()
+    erq[0:F, 0:32] = nt(
+        jnp.concatenate([ers[k] for k in range(NK)], axis=1),
+        jnp.concatenate([wds[k, UP:FP, :] for k in range(NK)], axis=1),
+    )
 
     @pl.loop(0, 4)
     def _(i):
@@ -237,7 +246,7 @@
     c_py = Exchange(py_r)
     for d in (1, 3, 2):
         c_py.send(pown, py_r.at[d - 1], to_y(d))
-    t1 = t_own(4, 2)
+    t1 = t_own(3, 2)
 
     dc[...] = dt[...].T.astype(BF)
     c_dc = send(dc, dcp, to_core)
@@ -249,10 +258,33 @@
         for n in range(4):
             rsf[i, n] = r[:, n * 128 : (n + 1) * 128]
 
-    t0[0].wait_recv()
-    t0[1].wait_recv()
-    far = [t_right(0, 2), t_left(2, 2)]
-    t2 = t_own(6, 1)
+    c_w.wait_recv()
+    c_dc.wait_recv()
+
+    def rs_peer(d):
+        i = wrap(x + d)
+        r = nn(dcp[0:256, :], jnp.concatenate([wsp[2 * i], wsp[2 * i + 1]], axis=1))
+        for n in range(4):
+            v = rsf[i, n, top] + r[:, n * 128 : (n + 1) * 128]
+            rsf[i, n, top] = v
+            rsp[i, n, top] = v.astype(BF)
+        i = wrap(z + d)
+        lanes = pl.ds(pl.multiple_of(lax.rem(i, 2) * 128, 128), 128)
+        w = [wsp[2 * n + i // 2, :, lanes] for n in range(4)]
+        r = nn(dcp[256:512, :], jnp.concatenate(w, axis=1))
+        for n in range(4):
+            v = rsf[n, i, bottom] + r[:, n * 128 : (n + 1) * 128]
+            rsf[n, i, bottom] = v
+            rsp[n, i, bottom] = v.astype(BF)
+
+    top, bottom = pl.ds(0, 256), pl.ds(256, 256)
+    x1, x2, x3 = wrap(x + 1), wrap(x + 2), wrap(x + 3)
+    z1, z2, z3 = wrap(z + 1), wrap(z + 2), wrap(z + 3)
+    q0, q1, q2, q3 = (pl.ds(n * 128, 128) for n in range(4))
+    c_ha, c_hb = Exchange(ha), Exchange(hb)
+    c_na, c_nb = Exchange(ra.at[pl.ds(0, 2)]), Exchange(rb.at[pl.ds(0, 2)])
+    c_ra, c_rb = Exchange(ra.at[pl.ds(2, 2)]), Exchange(rb.at[pl.ds(2, 2)])
+    rs_peer(2)
     c_py.wait_recv()
     pf[...] = ((pown[...] + py_r[1]) + (py_r[0] + py_r[2])) * 0.25
     base = core * 48 + z * 12
@@ -262,6 +294,10 @@
     c_pg = Exchange(pg.at[pl.ds(0, 45)])
     for i, j in PLANE:
         c_pg.send(pg.at[own], pg.at[own], to_plane(i, j))
+    c_ha.send(rsp.at[x2, :, q0], ha.at[0], to_x(1))
+    c_ha.send(rsp.at[x2, :, q1], ha.at[1], to_x(3))
+    c_hb.send(rsp.at[:, z2, q2], hb.at[0], to_z(1))
+    c_hb.send(rsp.at[:, z2, q3], hb.at[1], to_z(3))
     p3[...] = split3(pf[...])
     hp3 = split3(fold(nn(p3[:, 0:F], ht[...])))
 
@@ -276,17 +312,14 @@
     s_part(2 * core)
     s_part(2 * core + 1)
 
-    c_w.wait_recv()
-    c_dc.wait_recv()
-
-    def rs_peer(i):
-        r = nn(dcp[...], jnp.concatenate([wsp[2 * i], wsp[2 * i + 1]], axis=1))
-        for n in range(4):
-            v = rsf[i, n] + r[:, n * 128 : (n + 1) * 128]
-            rsf[i, n] = v
-            rsp[i, n] = v.astype(BF)
-
-    pl.loop(0, 2)(rs_peer)
+    t0[0].wait_recv()
+    far = [t_right(0, 2)]
+    t0[1].wait_recv()
+    far.append(t_left(2, 1))
+    t2 = t_own(5, 1)
+
+    rs_peer(1)
+    rs_peer(3)
     c_sc.wait_recv()
     half = pl.ds(16 * core, 16)
     sb[half] = sb[half] + sc_r[...]
@@ -295,34 +328,34 @@
         c_sp.send(
             sb.at[16 * core + 4 * wrap(x + i) + wrap(z + j)], sp_r.at[4 * i + j - 1], to_plane(i, j)
         )
-    pl.loop(2, 4)(rs_peer)
-    top, bottom = pl.ds(0, 256), pl.ds(256, 256)
-    c_r = {}
-
-    def bulk(j):
-        zj, xj = wrap(z + j), wrap(x + j)
-        c_r[j] = Exchange(rr.at[j])
-        for d in (1, 3, 2):
-            c_r[j].send(rsp.at[wrap(x + d), zj, top], rr.at[j, d - 1], to_x(d))
-            c_r[j].send(rsp.at[xj, wrap(z + d), bottom], rr.at[j, d + 2], to_z(d))
-
-    bulk(1)
-    bulk(2)
+    c_na.send(rsp.at[x1, :, q1], ra.at[0], to_x(1))
+    c_na.send(rsp.at[x3, :, q0], ra.at[1], to_x(3))
+    c_nb.send(rsp.at[:, z1, q3], rb.at[0], to_z(1))
+    c_nb.send(rsp.at[:, z3, q2], rb.at[1], to_z(3))
+    rs_peer(0)
+    t1[1].wait_recv()
+    far.append(t_left(3, 1))
     c_pg.wait_recv()
     own = pl.ds(core * 48, 48)
     c_pgc = send(pg.at[own], pg.at[own], to_core)
+    c_ha.wait_recv()
+    rsp[x1, :, q0] = (rsf[x1, :, q0] + ha[0].astype(F32)).astype(BF)
+    rsp[x3, :, q1] = (rsf[x3, :, q1] + ha[1].astype(F32)).astype(BF)
+    c_ra.send(rsp.at[x1, :, q0], ra.at[2], to_x(1))
+    c_ra.send(rsp.at[x3, :, q1], ra.at[3], to_x(3))
+
+    c_hb.wait_recv()
+    rsp[:, z1, q2] = (rsf[:, z1, q2] + hb[0].astype(F32)).astype(BF)
+    rsp[:, z3, q3] = (rsf[:, z3, q3] + hb[1].astype(F32)).astype(BF)
+    c_rb.send(rsp.at[:, z1, q2], rb.at[2], to_z(1))
+    c_rb.send(rsp.at[:, z3, q3], rb.at[3], to_z(3))
     c_sp.wait_recv()
     mine = core * 16 + x * 4 + z
     s2[...] = jnp.sum(sp_r[...], axis=0) + sb[mine]
     c_sy = Exchange(sy_r)
     for d in (1, 3, 2):
         c_sy.send(s2, sy_r.at[d - 1], to_y(d))
-    t3 = t_own(7, 1)
-    t1[0].wait_recv()
-    far.append(t_right(4, 1))
-    t1[1].wait_recv()
-    far.append(t_left(5, 1))
-
+    t3, t4 = t_own(6, 1), t_own(7, 1)
     c_pgc.wait_recv()
     for i in range(12):
         ct[:, i] = jnp.transpose(pg[8 * i : 8 * i + 8], (1, 0, 2))
@@ -345,6 +378,13 @@
         done_t.append(t * scale)
         tt[k : k + 1, :] = done_t[-1]
 
+    def m_part(k):
+        ms[k] = nn(ht[...], dys[k]) + ers[k].astype(F32)
+
+    pl.loop(0, 2)(m_part)
+    far.append(t_left(4, 1))
+    t2[0].wait_recv()
+    far.append(t_right(5, 1))
     c_sy.wait_recv()
     s = (s2[...] + sy_r[1]) + (sy_r[0] + sy_r[2])
     q = jnp.zeros((R, 128), F32)
@@ -354,38 +394,34 @@
     c_g = Exchange(sf.at[pl.ds(0, 15)])
     for i, j in PLANE:
         c_g.send(sf.at[mine], sf.at[mine], to_plane(i, j))
-    bulk(3)
-    bulk(0)
-    t2[0].wait_recv()
-    far.append(t_right(6, 1))
-
-    @pl.loop(0, NK)
-    def _(k):
-        ms[k] = nn(ht[...], dys[k]) + ers[k].astype(F32)
 
     c_zx = Exchange(zx)
 
-    def first_sums(j):
-        c_r[j].wait_recv()
-        a = rsf[x, wrap(z + j), top]
-        b = rsf[wrap(x + j), z, bottom]
-        for d in range(3):
-            a += rr[j, d].astype(F32)
-            b += rr[j, d + 3].astype(F32)
-        return a, b
-
-    def second(j):
-        a, b = first_sums(j)
-        a1[j] = a.astype(BF)
-        b1[j] = b.astype(BF)
+    def a_sum(n, lo, hi, j):
+        return rsf[x, j, pl.ds(n * 128, 128)] + (ra[lo, j].astype(F32) + ra[hi, j].astype(F32))
+
+    def b_sum(n, lo, hi, j):
+        return rsf[j, z, pl.ds(n * 128, 128)] + (rb[lo, j].astype(F32) + rb[hi, j].astype(F32))
+
+    c_na.wait_recv()
+    c_ra.wait_recv()
+    for j in (1, 3, 2):
+        zj = wrap(z + j)
+        a1[j, q0] = a_sum(0, 2, 1, zj).astype(BF)
+        a1[j, q1] = a_sum(1, 0, 3, zj).astype(BF)
         c_zx.send(a1.at[j], zx.at[j - 1], to_z(j))
+    c_nb.wait_recv()
+    c_rb.wait_recv()
+    for j in (1, 3, 2):
+        xj = wrap(x + j)
+        b1[j, q0] = b_sum(2, 2, 1, xj).astype(BF)
+        b1[j, q1] = b_sum(3, 0, 3, xj).astype(BF)
         c_zx.send(b1.at[j], zx.at[j + 2], to_x(j))
-
-    second(1)
-    second(2)
+    pl.loop(2, 4)(m_part)
     t3[1].wait_recv()
-    far.append(t_left(7, 1))
-
+    far.append(t_left(6, 1))
+    t4[0].wait_recv()
+    far.append(t_right(7, 1))
     p = jnp.zeros((R, FP), F32)
     for i in range(R):
         p += tt[:, i : i + 1] * pf[i : i + 1, :]
@@ -404,8 +440,17 @@
     c_gc = send(sf.at[own], sf.at[own], to_core)
     for i in range(16):
         right_part(core * 16 + i)
-    second(3)
-    a, b = first_sums(0)
+    def finals(j):
+        block, lo = j // 2, pl.multiple_of(lax.rem(j, 2) * 512, 512)
+        cols = pl.ds(pl.multiple_of(j * 512, 512), 512)
+        approx = nn(left[0:F, :], right[:, cols])
+        ne[:, cols] = (ms[block, :, pl.ds(lo, 512)] - approx).astype(BF)
+    @pl.loop(0, 4)
+    def _(j):
+        finals(core * 4 + j)
+
+    a = jnp.concatenate([a_sum(0, 2, 1, z), a_sum(1, 0, 3, z)], axis=0)
+    b = jnp.concatenate([b_sum(2, 2, 1, x), b_sum(3, 0, 3, x)], axis=0)
     c_gc.wait_recv()
     for i in range(16):
         right_part(other * 16 + i)
@@ -415,7 +460,7 @@
         b += zx[d + 3].astype(F32)
     igs[0:256, :] = a.astype(BF)
     igs[256:512, :] = b.astype(BF)
-    for c in (t2[1], t3[0], *far):
+    for c in (t1[0], t2[1], t3[0], t4[1], *far):
         c.wait_recv()
     for c in sent:
         c.wait_send()
@@ -434,75 +479,78 @@
         v((96, 8, 128), F32), v((8, 12, 8, 128), F32), v((8, 128), F32),
         v((32, 8, 128), F32), v((16, 8, 128), F32), v((15, 8, 128), F32),
         v((8, 128), F32), v((3, 8, 128), F32), v((32, 8, 128), F32),
-        v((4, 4, TOK, 128), F32), v((4, 4, TOK, 128), BF), v((4, 6, 256, 128), BF),
+        v((4, 4, TOK, 128), F32), v((4, 4, TOK, 128), BF),
+        v((2, 4, 128, 128), BF), v((2, 4, 128, 128), BF),
+        v((4, 4, 128, 128), BF), v((4, 4, 128, 128), BF),
         v((4, 256, 128), BF), v((4, 256, 128), BF), v((6, 256, 128), BF),
-        pltpu.SemaphoreType.DMA((35,)),
+        pltpu.SemaphoreType.DMA((21,)),
         pltpu.SemaphoreType.DMA((N_SEM,)),
         pltpu.SemaphoreType.DMA((N_SEM,)),
     ]
     out_shape = (
-        v((TOK, 128), BF), v((4, 8, F, 128), BF), v((NK, F, KC), F32), v((F, KC), F32),
-        v((FP, 128), BF), v((128, D), BF),
+        v((TOK, 128), BF), v((F, D), BF), v((4, 8, F, 128), BF),
+        v((NK, F, KC), F32), v((F, KC), F32), v((FP, 128), BF), v((128, D), BF),
     )
     return pl.pallas_call(
         step_kernel,
         out_shape=out_shape,
         in_specs=[any_spec] * 8,
-        out_specs=[vmem_spec] * 6,
+        out_specs=[vmem_spec] * 7,
         scratch_shapes=scratch,
         compiler_params=pltpu.CompilerParams(
-            collective_id=0, has_side_effects=True, vmem_limit_bytes=48 * 1024 * 1024
+            collective_id=0, has_side_effects=True, vmem_limit_bytes=42 * 1024 * 1024
         ),
         name="exchange",
     )(x, dy, wg, wu, wd, er, mo, q)
 
 
-def apply_kernel(ig, t_ref, m_ref, mo_ref, left, right, ig_o, nd_o, ne_o, nm_o, nd, ne, nm, sem):
+def store_kernel(
+    ig, ne, tg, ms, mos, left, right, ig_o, nd_o, ne_o, nm_o, nd, ne2, nm, sem
+):
     dp = lax.axis_index("dp")
-    out_ig = pltpu.make_async_copy(ig, ig_o, sem.at[0])
-    out_ig.start()
-    l = left[0:F, :]
-    copies = [out_ig]
+    core = lax.rem(lax.axis_index("mp"), 2)
+    copies = []
+
+    def out(src, dst):
+        copies.append(pltpu.make_async_copy(src, dst, sem.at[len(copies)]))
+        copies[-1].start()
+
+    def at(block, n):
+        return pl.ds(pl.multiple_of(block * 512, 512), n * 512)
+
+    for n in range(2):
+        cols = at(core * 4 + 2 * n, 2)
+        out(ne.at[:, cols], ne_o.at[:, cols])
+    out(ig, ig_o)
+    factor = left[0:F, :]
     for j in range(8):
+        block = (1 - core) * 4 + j if j < 4 else core * 4 + j - 4
+        chunk = (1 - core) * 2 + j // 2 if j < 4 else core * 2 + (j - 4) // 2
+        approx = nn(factor, right[:, at(block, 1)])
         cols = slice(j * 512, (j + 1) * 512)
-        approx = nn(l, right[:, cols])
-        half = slice((j % 2) * 512, (j % 2) * 512 + 512)
-        ne[:, cols] = (m_ref[j // 2, :, half] - approx).astype(BF)
+        half = slice((j % 2) * 512, (j % 2 + 1) * 512)
+        if j < 4:
+            ne2[:, cols] = (ms[chunk, :, half] - approx).astype(BF)
+            out(ne2.at[:, cols], ne_o.at[:, at(block, 1)])
         for c in range(4):
-            lanes = slice(c * 128, (c + 1) * 128)
-            b = 4 * j + c
-            nd[:, b * 128 : (b + 1) * 128] = (
-                t_ref[b // 8, b % 8].astype(F32) - 0.1 * approx[:, lanes]
+            t = tg[chunk, (j % 2) * 4 + c].astype(F32)
+            nd[:, j * 512 + c * 128 : j * 512 + (c + 1) * 128] = (
+                t - 0.1 * approx[:, c * 128 : (c + 1) * 128]
             ).astype(BF)
-        for n, (src, dst) in enumerate(((ne, ne_o), (nd, nd_o))):
-            copies.append(
-                pltpu.make_async_copy(
-                    src.at[:, pl.ds(j * 512, 512)], dst.at[:, pl.ds(j * 512, 512)],
-                    sem.at[1 + 2 * j + n],
-                )
-            )
-            copies[-1].start()
-        if j % 4 == 1:
-            h = j // 4
-            cols = pl.ds(pl.multiple_of(dp * KC + h * 512, 512), 512)
-            nm[:, h * 512 : (h + 1) * 512] = 0.9 * mo_ref[:, h * 512 : (h + 1) * 512] + nn(
-                l, right[:, cols]
-            )
-            copies.append(
-                pltpu.make_async_copy(
-                    nm.at[:, pl.ds(h * 512, 512)], nm_o.at[:, pl.ds(h * 512, 512)], sem.at[17 + h]
-                )
-            )
-            copies[-1].start()
+        out(nd.at[:, cols], nd_o.at[:, at(block, 1)])
+        if j < 2:
+            cols = slice(j * 512, (j + 1) * 512)
+            nm[:, cols] = 0.9 * mos[:, cols] + nn(factor, right[:, at(2 * dp + j, 1)])
+            out(nm.at[:, cols], nm_o.at[:, cols])
     for c in copies:
         c.wait()
 
 
-def apply(*args):
+def store(*args):
     v = pltpu.VMEM
     args = [pltpu.with_memory_space_constraint(a, pltpu.VMEM) for a in args]
     return pl.pallas_call(
-        apply_kernel,
+        store_kernel,
         out_shape=(
             jax.ShapeDtypeStruct((TOK, 128), BF),
             jax.ShapeDtypeStruct((F, D), BF),
@@ -512,10 +560,10 @@
         in_specs=[pl.BlockSpec(memory_space=pltpu.VMEM)] * len(args),
         out_specs=[pl.BlockSpec(memory_space=pl.ANY)] * 4,
         scratch_shapes=[
-            v((F, D), BF), v((F, D), BF), v((F, KC), F32), pltpu.SemaphoreType.DMA((20,)),
+            v((F, D), BF), v((F, D // 2), BF), v((F, KC), F32), pltpu.SemaphoreType.DMA((17,)),
         ],
-        compiler_params=pltpu.CompilerParams(vmem_limit_bytes=24 * 1024 * 1024),
-        name="apply",
+        compiler_params=pltpu.CompilerParams(vmem_limit_bytes=20 * 1024 * 1024),
+        name="store",
     )(*args)
 
 
@@ -523,7 +571,7 @@
     kept = exchange(
         inputs, out_grads, w_gate.T, w_up.T, w_down, err_down[0], mom_down, q_down.T
     )
-    ig, nd, ne, nm = apply(*kept)
+    ig, nd, ne, nm = store(*kept)
     return ig, nd, ne[None], nm
 
 

time: 45.8 us -> 43 us (0.939); the launches traced: 45.7 us -> 42.3 us
  Pallas kernels: 45 us -> 41.7 us
    pallas_call x1, Pallas kernels: 41.7 us -> 38.6 us  [exchange(): pl.pallas_call(step_kernel, out_shape=out_shape, in_specs=[any_spec] * 8,...]
where the time goes in v4:
time: 43 us; the launch traced here: 42.3 us
  Pallas kernels  41.7 us (97%)
  between operations  0.64 us (1%)
    pallas_call x1, Pallas kernels, exchange(): pl.pallas_call(step_kernel, out_shape=out_shape, in_specs=[any_spec] * 8,...  38.6 us
    pallas_call x1, Pallas kernels, store(): pl.pallas_call(store_kernel, out_shape=(jax.ShapeDtypeStruct((TOK, 128),...  3.1 us

profile of v4, /device:TPU:0, one launch (start us, length us, event | category | flops | bytes accessed | tf_op | source)
XLA Modules:
  0.0 42.3 jit_solution(16432268915536123427)
XLA Ops:
  0.6 38.6 %exchange.1 = (bf16[512,128]{1,0:T(8,128)(2,1)S(1)}, bf16[344,4096]{1,0:T(8,128)(2,1)S(1)}, bf16[4,8,344,128]{3,2,1,0:T(8,128)(2,1)S(1)}, f32[4,344,1024]{2,1,0:...) custom-call(bf16[512,4096]{1,0:T(8,128)(2,1)} %x_h.1, ...), custom_call_target="tpu_custom_call" | custom-call | tf_op jit(solution)/shard_map/exchange/pallas_call | solution.py:494
  39.2 3.1 %store.1 = (bf16[512,128]{1,0:T(8,128)(2,1)}, bf16[344,4096]{1,0:T(8,128)(2,1)}, bf16[344,4096]{1,0:T(8,128)(2,1)}, f32[344,1024]{1,0:T(8,128)}) custom-call(bf16[512,128]{1,0:T(8,128)(2,1)S(1)} %get-tuple-element.15.ig, bf16[344,4096]{1,0:T(8,128)(2,1)S(1)} %get-tuple-element.16.ne, bf16[4,8,344,128]{3,2,1,0:T(8,128)(2,1)S(1)} %get-tuple-element.17.tg, ...), custom_call_target="tpu_custom_call" | custom-call | tf_op jit(solution)/shard_map/store/pallas_call | solution.py:552

commit v5 on v4

--- a/solution.py
+++ b/solution.py
@@ -47,7 +47,7 @@
 
 def step_kernel(
     x_h, dy_h, wg_h, wu_h, wd_h, er_h, mo_h, q_h,
-    igs, ne, tg, ms, mos, left, right,
+    igs, tg, ms, mos, left, right,
     xs, dys, ws, wds, ers, qs, wsp,
     gu, dhq, ht, dt, dc, dcp, erq,
     pown, py_r, p3, pf, pg, ct, tt,
@@ -440,15 +440,6 @@
     c_gc = send(sf.at[own], sf.at[own], to_core)
     for i in range(16):
         right_part(core * 16 + i)
-    def finals(j):
-        block, lo = j // 2, pl.multiple_of(lax.rem(j, 2) * 512, 512)
-        cols = pl.ds(pl.multiple_of(j * 512, 512), 512)
-        approx = nn(left[0:F, :], right[:, cols])
-        ne[:, cols] = (ms[block, :, pl.ds(lo, 512)] - approx).astype(BF)
-    @pl.loop(0, 4)
-    def _(j):
-        finals(core * 4 + j)
-
     a = jnp.concatenate([a_sum(0, 2, 1, z), a_sum(1, 0, 3, z)], axis=0)
     b = jnp.concatenate([b_sum(2, 2, 1, x), b_sum(3, 0, 3, x)], axis=0)
     c_gc.wait_recv()
@@ -488,14 +479,14 @@
         pltpu.SemaphoreType.DMA((N_SEM,)),
     ]
     out_shape = (
-        v((TOK, 128), BF), v((F, D), BF), v((4, 8, F, 128), BF),
+        v((TOK, 128), BF), v((4, 8, F, 128), BF),
         v((NK, F, KC), F32), v((F, KC), F32), v((FP, 128), BF), v((128, D), BF),
     )
     return pl.pallas_call(
         step_kernel,
         out_shape=out_shape,
         in_specs=[any_spec] * 8,
-        out_specs=[vmem_spec] * 7,
+        out_specs=[vmem_spec] * 6,
         scratch_shapes=scratch,
         compiler_params=pltpu.CompilerParams(
             collective_id=0, has_side_effects=True, vmem_limit_bytes=42 * 1024 * 1024
@@ -505,42 +496,31 @@
 
 
 def store_kernel(
-    ig, ne, tg, ms, mos, left, right, ig_o, nd_o, ne_o, nm_o, nd, ne2, nm, sem
+    ig, tg, ms, mos, left, right, ig_o, nd_o, ne_o, nm_o, nd, ne, nm, sem
 ):
     dp = lax.axis_index("dp")
-    core = lax.rem(lax.axis_index("mp"), 2)
     copies = []
 
     def out(src, dst):
         copies.append(pltpu.make_async_copy(src, dst, sem.at[len(copies)]))
         copies[-1].start()
 
-    def at(block, n):
-        return pl.ds(pl.multiple_of(block * 512, 512), n * 512)
-
-    for n in range(2):
-        cols = at(core * 4 + 2 * n, 2)
-        out(ne.at[:, cols], ne_o.at[:, cols])
     out(ig, ig_o)
     factor = left[0:F, :]
     for j in range(8):
-        block = (1 - core) * 4 + j if j < 4 else core * 4 + j - 4
-        chunk = (1 - core) * 2 + j // 2 if j < 4 else core * 2 + (j - 4) // 2
-        approx = nn(factor, right[:, at(block, 1)])
         cols = slice(j * 512, (j + 1) * 512)
-        half = slice((j % 2) * 512, (j % 2 + 1) * 512)
-        if j < 4:
-            ne2[:, cols] = (ms[chunk, :, half] - approx).astype(BF)
-            out(ne2.at[:, cols], ne_o.at[:, at(block, 1)])
+        approx = nn(factor, right[:, cols])
+        ne[:, cols] = (ms[j // 2, :, (j % 2) * 512 : (j % 2 + 1) * 512] - approx).astype(BF)
+        out(ne.at[:, cols], ne_o.at[:, cols])
         for c in range(4):
-            t = tg[chunk, (j % 2) * 4 + c].astype(F32)
+            t = tg[j // 2, (j % 2) * 4 + c].astype(F32)
             nd[:, j * 512 + c * 128 : j * 512 + (c + 1) * 128] = (
                 t - 0.1 * approx[:, c * 128 : (c + 1) * 128]
             ).astype(BF)
-        out(nd.at[:, cols], nd_o.at[:, at(block, 1)])
+        out(nd.at[:, cols], nd_o.at[:, cols])
         if j < 2:
-            cols = slice(j * 512, (j + 1) * 512)
-            nm[:, cols] = 0.9 * mos[:, cols] + nn(factor, right[:, at(2 * dp + j, 1)])
+            own = pl.ds(pl.multiple_of(dp * KC + j * 512, 512), 512)
+            nm[:, cols] = 0.9 * mos[:, cols] + nn(factor, right[:, own])
             out(nm.at[:, cols], nm_o.at[:, cols])
     for c in copies:
         c.wait()
@@ -560,7 +540,7 @@
         in_specs=[pl.BlockSpec(memory_space=pltpu.VMEM)] * len(args),
         out_specs=[pl.BlockSpec(memory_space=pl.ANY)] * 4,
         scratch_shapes=[
-            v((F, D), BF), v((F, D // 2), BF), v((F, KC), F32), pltpu.SemaphoreType.DMA((17,)),
+            v((F, D), BF), v((F, D), BF), v((F, KC), F32), pltpu.SemaphoreType.DMA((19,)),
         ],
         compiler_params=pltpu.CompilerParams(vmem_limit_bytes=20 * 1024 * 1024),
         name="store",

time: 43 us -> 43.9 us (1.021)
  local copies, waits for them, and re-layouts: 0 us -> 0.9 us
    unnamed x0 -> x2, local copies, waits for them, and re-layouts: none -> 0.9 us
where the time goes in v5:
time: 43.9 us; the launch traced here: 43.2 us
  Pallas kernels  41.7 us (95%)
  local copies, waits for them, and re-layouts  0.9 us (2%)
  between operations  0.65 us (1%)
    pallas_call x1, Pallas kernels, exchange(): pl.pallas_call(step_kernel, out_shape=out_shape, in_specs=[any_spec] * 8,...  38.3 us
    pallas_call x1, Pallas kernels, store(): pl.pallas_call(store_kernel, out_shape=(jax.ShapeDtypeStruct((TOK, 128),...  3.34 us
    unnamed x2, local copies, waits for them, and re-layouts  0.9 us

profile of v5, /device:TPU:0, one launch (start us, length us, event | category | flops | bytes accessed | tf_op | source)
XLA Modules:
  0.0 43.2 jit_solution(11831885994497002760)
XLA Ops:
  0.6 0.0 copy-start
  0.6 0.9 %copy-done = f32[4096,8]{0,1:T(8,128)S(1)} copy-done((f32[4096,8]{0,1:T(8,128)S(1)}, f32[4096,8]{0,1:T(8,128)}, u32[]{:S(2)}) %copy-start) | copy-done | bytes 131096
  1.5 38.3 %exchange.1 = (bf16[512,128]{1,0:T(8,128)(2,1)S(1)}, bf16[4,8,344,128]{3,2,1,0:T(8,128)(2,1)S(1)}, f32[4,344,1024]{2,1,0:T(8,128)S(1)}, f32[344,1024]{1,0:T(8,12...) custom-call(bf16[512,4096]{1,0:T(8,128)(2,1)} %x_h.1, bf16[512,4096]{1,0:T(8,128)(2,1)} %dy_h.1, ...), custom_call_target="tpu_custom_call" | custom-call | tf_op jit(solution)/shard_map/exchange/pallas_call | solution.py:485
  39.9 3.3 %store.1 = (bf16[512,128]{1,0:T(8,128)(2,1)}, bf16[344,4096]{1,0:T(8,128)(2,1)}, bf16[344,4096]{1,0:T(8,128)(2,1)}, f32[344,1024]{1,0:T(8,128)}) custom-call(bf16[512,128]{1,0:T(8,128)(2,1)S(1)} %get-tuple-element.14.ig, bf16[4,8,344,128]{3,2,1,0:T(8,128)(2,1)S(1)} %get-tuple-element.15.tg, f32[4,344,1024]{2,1,0:T(8,128)S(1)} %get-tuple-element.16.ms, ...), custom_call_target="tpu_custom_call" | custom-call | tf_op jit(solution)/shard_map/store/pallas_call | solution.py:532
Async XLA Ops:
  0.6 0.9 %copy-start = (f32[4096,8]{0,1:T(8,128)S(1)}, f32[4096,8]{0,1:T(8,128)}, u32[]{:S(2)}) copy-start(f32[4096,8]{0,1:T(8,128)} %param.15) | copy-start | bytes 393220
